TPU v7x, 32 devices: a whole 2x2x4 slice. The times are simulated.
32 devices in a mesh: dp: 8 (over y, x, core), fsdp: 4 (over z).
Axes of the slice: x: 2, y: 2, z: 4, core: 2. Of those that a mesh axis runs over, the one named last changes fastest.
Arguments:
- tokens: bfloat16 [16384, 1024], P(('dp', 'fsdp')), may hold values from -20 to 20
- w_qkv: bfloat16 [1024, 3072], P('fsdp'), may hold values from -0.1875 to 0.1875
- w_out: bfloat16 [1024, 1024], P('fsdp'), may hold values from -0.1875 to 0.1875
- doc_blocks: int32 [32, 4], P(('dp', 'fsdp')), may hold values from 0 to 1, never falling along the last dimension, each value on 1 to 3 neighbouring positions
- cotangent: bfloat16 [16384, 1024], P(('dp', 'fsdp')), may hold values from -6 to 6
Outputs:
- output: bfloat16 [16384, 1024], P(('dp', 'fsdp'))
- grad_tokens: bfloat16 [16384, 1024], P(('dp', 'fsdp'))
- grad_w_qkv: float32 [1024, 3072], P('fsdp')
- grad_w_out: float32 [1024, 1024], P('fsdp')
Inputs may be any that keep to these rules, and one draw needn't show every extreme that they name: `doc_blocks`: ids never fall along a sequence; each of the 2 documents of a sequence covers 1 to 3 blocks.
All inputs are finite; a program needn't handle non-finite values.
Results may differ from a plain program's by a relative error of at most 0.012.
Values may be sent and summed in bfloat16 or wider, within the bound.
A program may use at most 128 MiB of HBM per device.

v0:
```python
import math

import jax
import jax.numpy as jnp
from jax import lax
from jax.sharding import PartitionSpec as P

H = 8


NEG_FILL = -1e30
CONTRACT_ROWS = (((0,), (0,)), ((), ()))
CONTRACT_COLS = (((1,), (1,)), ((), ()))


def row_mask(doc_ids, row_count):
    block_len = row_count // doc_ids.shape[0]
    doc_rows = jnp.repeat(doc_ids, block_len, total_repeat_length=row_count)
    position = jnp.arange(row_count, dtype=jnp.int32)
    causal = position[None, :] <= position[:, None]
    return causal & (doc_rows[None, :] == doc_rows[:, None])


def split_heads(matrix, head_count):
    return matrix.reshape(matrix.shape[0], head_count, matrix.shape[1] // head_count)


def attend_forward(query_rows, key_rows, value_rows, allowed, head_count):
    row_count = query_rows.shape[0]
    query_heads = split_heads(query_rows, head_count)
    key_heads = split_heads(key_rows, head_count)
    value_heads = split_heads(value_rows, head_count)
    score_scale = query_heads.shape[2] ** (-0.5)
    scores = (
        jnp.einsum("qhd,khd->hqk", query_heads, key_heads, preferred_element_type=jnp.float32)
        * score_scale
    )
    scores = jnp.where(allowed[None], scores, NEG_FILL)
    highest = jnp.max(scores, axis=-1, keepdims=True)
    expvals = jnp.exp(scores - highest)
    attn_probs = expvals / jnp.sum(expvals, axis=-1, keepdims=True)
    probs_half = attn_probs.astype(jnp.bfloat16)
    mixed = jnp.einsum("hqk,khd->qhd", probs_half, value_heads, preferred_element_type=jnp.float32)
    return (mixed.astype(jnp.bfloat16).reshape(row_count, -1), attn_probs, probs_half)


def attend_backward(
    query_rows, key_rows, value_rows, attn_probs, probs_half, grad_mixed, head_count
):
    row_count = query_rows.shape[0]
    query_heads = split_heads(query_rows, head_count)
    key_heads = split_heads(key_rows, head_count)
    value_heads = split_heads(value_rows, head_count)
    grad_heads = split_heads(grad_mixed, head_count)
    score_scale = query_heads.shape[2] ** (-0.5)
    grad_probs = jnp.einsum(
        "qhd,khd->hqk", grad_heads, value_heads, preferred_element_type=jnp.float32
    )
    grad_values = jnp.einsum(
        "hqk,qhd->khd", probs_half, grad_heads, preferred_element_type=jnp.float32
    )
    inner = jnp.sum(attn_probs * grad_probs, axis=-1, keepdims=True)
    grad_scores = (attn_probs * (grad_probs - inner)).astype(jnp.bfloat16)
    grad_queries = (
        jnp.einsum("hqk,khd->qhd", grad_scores, key_heads, preferred_element_type=jnp.float32)
        * score_scale
    )
    grad_keys = (
        jnp.einsum("hqk,qhd->khd", grad_scores, query_heads, preferred_element_type=jnp.float32)
        * score_scale
    )
    pieces_list = [grad_queries, grad_keys, grad_values]
    return jnp.concatenate(
        [p.astype(jnp.bfloat16).reshape(row_count, -1) for p in pieces_list], axis=1
    )


def body(tokens, w_qkv, w_out, doc_blocks, cotangent):
    row_count = tokens.shape[0]
    head_width = w_out.shape[1]
    head_count = H
    all_devices = lax.axis_size("dp") * lax.axis_size("fsdp")
    allowed = row_mask(doc_blocks[0], row_count)
    columns = tokens
    qkv = jnp.dot(
        columns,
        lax.all_gather(w_qkv, "fsdp", axis=0, tiled=True),
        preferred_element_type=jnp.float32,
    ).astype(jnp.bfloat16)
    query_rows = qkv[:, :head_width]
    key_rows = qkv[:, head_width : 2 * head_width]
    value_rows = qkv[:, 2 * head_width :]
    mixed, attn_probs, probs_half = attend_forward(
        query_rows, key_rows, value_rows, allowed, head_count
    )
    output = lax.dot_general(
        mixed,
        lax.all_gather(w_out, "fsdp", axis=0, tiled=True),
        CONTRACT_COLS,
        preferred_element_type=jnp.float32,
    )
    columns = cotangent
    grad_mixed = jnp.dot(
        columns,
        lax.all_gather(w_out, "fsdp", axis=0, tiled=True),
        preferred_element_type=jnp.float32,
    ).astype(jnp.bfloat16)
    output = output.astype(jnp.bfloat16)
    grad_qkv = attend_backward(
        query_rows, key_rows, value_rows, attn_probs, probs_half, grad_mixed, head_count
    )
    grad_tokens = lax.dot_general(
        grad_qkv,
        lax.all_gather(w_qkv, "fsdp", axis=0, tiled=True),
        CONTRACT_COLS,
        preferred_element_type=jnp.float32,
    )
    grad_tokens = grad_tokens.astype(jnp.bfloat16)
    first_term = lax.dot_general(
        tokens, grad_qkv, CONTRACT_ROWS, preferred_element_type=jnp.float32
    )
    second_term = lax.dot_general(
        cotangent, mixed, CONTRACT_ROWS, preferred_element_type=jnp.float32
    )
    partial_grad = lax.psum_scatter(
        jnp.concatenate([first_term, second_term], axis=1), "fsdp", scatter_dimension=0, tiled=True
    )
    summed = lax.psum(partial_grad, "dp")
    norm_factor = 1.0 / math.sqrt(row_count * all_devices)
    grad_w_qkv = summed[:, : 3 * head_width] * norm_factor
    grad_w_out = summed[:, 3 * head_width :] * norm_factor
    return (output, grad_tokens, grad_w_qkv, grad_w_out)


def solution(mesh):
    placed = (
        P(("dp", "fsdp"), None),
        P("fsdp", None),
        P("fsdp", None),
        P(("dp", "fsdp"), None),
        P(("dp", "fsdp"), None),
    )
    return jax.shard_map(
        body,
        mesh=mesh,
        in_specs=placed,
        out_specs=(
            P(("dp", "fsdp"), None),
            P(("dp", "fsdp"), None),
            P("fsdp", None),
            P("fsdp", None),
        ),
        check_vma=False,
    )
```

profile of v0, /device:TPU:0, one launch (start us, length us, event | category | flops | bytes accessed | tf_op | source)
XLA Modules:
  0.0 596.9 jit_solution(12965069515736910643)
XLA Ops:
  7.2 0.0 copy-start
  7.2 0.0 all-gather.5.cloned.1.call-start
  7.2 0.7 all-gather.5.cloned.1.call-update
  7.9 0.0 all-gather.3.cloned.1.call-start
  8.0 0.7 all-gather.3.cloned.1.call-update
  8.7 0.0 reduce-scatter.2.cloned.1.call-start
  8.7 1.4 fusion.30
  10.1 2.6 compare_select_fusion.1
  12.7 0.2 fusion.18
  13.0 45.0 %all-gather.5.cloned.1.call-done = bf16[1024,1024]{1,0:T(8,128)(2,1)} async-done(((bf16[256,1024]{1,0:T(8,128)(2,1)}), bf16[1024,1024]{1,0:T(8,128)(2,1)}) %all-gather.5.cloned.1.call-update) | async-done | bytes 2097168 | tf_op jit(solution)/shard_map/all_gather | solution.py:98
  58.0 3.2 convolution_convert_fusion.1
  61.1 1.3 copy.29
  62.5 111.2 %all-gather.3.cloned.1.call-done = bf16[1024,3072]{1,0:T(8,128)(2,1)} async-done(((bf16[256,3072]{1,0:T(8,128)(2,1)}), bf16[1024,3072]{1,0:T(8,128)(2,1)}) %all-gather.3.cloned.1.call-update) | async-done | bytes 6291472 | tf_op jit(solution)/shard_map/all_gather | solution.py:87
  173.7 0.0 copy-done
  173.7 6.4 %convolution_convert_fusion = bf16[512,3072]{1,0:T(8,128)(2,1)S(1)} fusion(bf16[512,1024]{1,0:T(8,128)(2,1)S(1)} %copy-done, bf16[1024,3072]{1,0:T(8,128)(2,1)} %all-gather.3.cloned.1.call-done), kind=kOutput, calls=%fused_computation.8 | convolution fusion | flops 3222798336 | bytes 10485760 | tf_op jit(solution)/shard_map/dot_general | solution.py:85
  180.1 1.8 fusion.29
  181.9 0.5 copy.27
  182.5 1.5 copy.28
  184.0 5.4 fusion.31
  189.4 0.0 copy-start.1
  189.4 0.0 copy-start.2
  189.4 4.7 fusion.9
  194.1 0.0 copy-start.9
  194.2 1.7 copy-done.1
  195.9 0.2 copy-done.2
  196.1 0.0 copy-start.5
  196.1 1.5 fusion.12
  197.6 0.0 copy-done.5
  197.6 0.0 copy-start.7
  197.7 1.5 multiply_reduce_fusion
  199.2 2.7 multiply_convert_fusion
  201.9 1.5 multiply_convert_fusion.1
  203.4 0.0 copy-start.3
  203.4 0.0 copy-start.6
  203.4 0.7 multiply_convert_fusion.2
  204.1 0.0 copy-done.9
  204.1 0.9 copy-done.6
  205.0 1.3 convolution_bitcast_fusion.1
  206.3 0.0 copy-done.7
  206.3 0.0 copy-done.3
  206.3 3.5 convolution_bitcast_fusion
  209.8 7.2 %pad_maximum_fusion = f32[1024,4096]{0,1:T(8,128)} fusion(f32[1024,1024]{0,1:T(8,128)S(1)} %convolution_bitcast_fusion.1, f32[1024,3072]{0,1:T(8,128)S(1)} %convolution_bitcast_fusion), kind=kLoop, calls=%fused_computation.1 | loop fusion | flops 4194304 | bytes 33554432 | tf_op jit(solution)/shard_map/concatenate | solution.py:126
  217.1 0.0 reduce-scatter.2.cloned.1.call-update
  217.1 0.0 copy-start.10
  217.1 0.0 all-reduce.2.cloned.1.call-start
  217.2 278.7 %reduce-scatter.2.cloned.1.call-done = f32[256,4096]{0,1:T(8,128)} async-done(((f32[1024,4096]{0,1:T(8,128)}), f32[256,4096]{0,1:T(8,128)}) %reduce-scatter.2.cloned.1.call-update) | async-done | bytes 4194320 | tf_op jit(solution)/shard_map/reduce_scatter | solution.py:125
  495.8 0.0 all-reduce.2.cloned.1.call-update
  495.9 0.0 copy-done.10
  495.9 0.0 copy-start.4
  495.9 0.0 copy-start.8
  495.9 4.0 convolution_convert_fusion.2
  499.9 0.0 copy-done.4
  499.9 0.0 copy-done.8
  499.9 7.2 %convolution_convert_fusion.3 = bf16[512,1024]{1,0:T(8,128)(2,1)} fusion(bf16[1024,3072]{1,0:T(8,128)(2,1)} %all-gather.3.cloned.1.call-done, bf16[512,1024]{0,1:T(8,128)(2,1)S(1)} %bitcast.77, bf16[512,1024]{0,1:T(8,128)(2,1)S(1)} %bitcast.70, bf16[512,1024]{0,1:T(8,128)(2,1)S(1)} %bitcast.72), kind=kOutput, calls=%fused_computation.26 | convolution fusion | flops 3231186944 | bytes 10485760 | tf_op jit(solution)/shard_map/dot_general | solution.py:112
  507.1 73.3 %all-reduce.2.cloned.1.call-done = f32[256,4096]{0,1:T(8,128)} async-done(((f32[256,4096]{0,1:T(8,128)}), f32[256,4096]{0,1:T(8,128)}) %all-reduce.2.cloned.1.call-update) | async-done | bytes 4194320 | tf_op jit(solution)/shard_map/psum | solution.py:128
  580.4 3.8 slice_multiply_fusion
  584.2 3.5 copy.21
  587.8 1.3 slice_multiply_fusion.1
  589.1 1.3 copy.22
  (3 shorter events, 0.0 us)
Async XLA Ops:
  7.2 166.5 %copy-start = (bf16[512,1024]{1,0:T(8,128)(2,1)S(1)}, bf16[512,1024]{1,0:T(8,128)(2,1)}, u32[]{:S(2)}) copy-start(bf16[512,1024]{1,0:T(8,128)(2,1)} %param.7) | copy-start | bytes 3145732
  7.2 50.8 %all-gather.5.cloned.1.call-start = ((), (), s32[]{:S(2)}) async-start(), calls=%async_computation.2 | async-start | bytes 2621440 | tf_op jit(solution)/shard_map/all_gather | solution.py:98
  7.9 165.8 %all-gather.3.cloned.1.call-start = ((), (), s32[]{:S(2)}) async-start(), calls=%async_computation.1 | async-start | bytes 7864320 | tf_op jit(solution)/shard_map/all_gather | solution.py:87
  8.7 487.2 %reduce-scatter.2.cloned.1.call-start = ((), (), s32[]{:S(2)}) async-start(), calls=%async_computation.3 | async-start | bytes 20971520 | tf_op jit(solution)/shard_map/reduce_scatter | solution.py:125
  189.4 6.5 %copy-start.1 = (f32[8,512,512]{1,2,0:T(8,128)S(1)}, f32[8,512,512]{1,2,0:T(8,128)}, u32[]{:S(2)}) copy-start(f32[8,512,512]{1,2,0:T(8,128)} %get-tuple-element.28) | copy-start | bytes 25165828
  189.4 6.7 %copy-start.2 = (bf16[512,1024]{0,1:T(8,128)(2,1)S(1)}, bf16[512,1024]{0,1:T(8,128)(2,1)}, u32[]{:S(2)}) copy-start(bf16[512,1024]{0,1:T(8,128)(2,1)} %copy.29) | copy-start | bytes 3145732
  194.1 10.0 %copy-start.9 = (bf16[8,128,512]{2,1,0:T(8,128)(2,1)}, bf16[8,128,512]{2,1,0:T(8,128)(2,1)S(1)}, u32[]{:S(2)}) copy-start(bf16[8,128,512]{2,1,0:T(8,128)(2,1)S(1)} %fusion.9) | copy-start | bytes 3145732
  196.1 1.5 copy-start.5
  197.6 8.6 %copy-start.7 = (bf16[8,128,512]{2,1,0:T(8,128)(2,1)}, bf16[8,128,512]{2,1,0:T(8,128)(2,1)S(1)}, u32[]{:S(2)}) copy-start(bf16[8,128,512]{2,1,0:T(8,128)(2,1)S(1)} %fusion.12) | copy-start | bytes 3145732
  203.4 2.9 copy-start.3
  203.4 1.6 copy-start.6
  217.1 278.8 %copy-start.10 = (bf16[8,128,512]{2,1,0:T(8,128)(2,1)S(1)}, bf16[8,128,512]{2,1,0:T(8,128)(2,1)}, u32[]{:S(2)}) copy-start(bf16[8,128,512]{2,1,0:T(8,128)(2,1)} %copy-done.9) | copy-start | bytes 3145732
  217.1 363.3 %all-reduce.2.cloned.1.call-start = ((), (), s32[]{:S(2)}) async-start(), calls=%async_computation.4 | async-start | bytes 8388608 | tf_op jit(solution)/shard_map/psum | solution.py:128
  495.9 4.0 copy-start.4
  495.9 4.0 copy-start.8
Sparse Core Ops, SparseCore 0:
  9.6 48.3 all-gather.4
  59.5 114.1 all-gather.2
  217.2 278.5 reduce-scatter.1
  499.0 81.4 all-reduce.1
where the time goes:
time: 597 us
  waiting for transfers between devices  510 us (85%)
  matrix products  41 us (7%)
  other arithmetic  17.8 us (3%)
  local copies, waits for them, and re-layouts  14.3 us (2%)
  between operations  14 us (2%)
    reduce_scatter x1, waiting for transfers between devices, body(): lax.psum_scatter(jnp.concatenate([first_term, second_term], axis=1), 'fsd...  279 us
    all_gather x1, waiting for transfers between devices, body(): lax.all_gather(w_qkv, 'fsdp', axis=0, tiled=True)  111 us
    psum x1, waiting for transfers between devices, body(): summed = lax.psum(partial_grad, 'dp')  73.3 us
    all_gather x1, waiting for transfers between devices, body(): lax.all_gather(w_out, 'fsdp', axis=0, tiled=True)  45 us
  transfers between devices with their start and end apart: 4, of which 4 were waited for; matrix products, arithmetic and copies ran while one was open for 3% of the time, Pallas kernels for 0%

commit v1 on v0

--- a/solution.py
+++ b/solution.py
@@ -1,8 +1,11 @@
+import functools
 import math
 
 import jax
 import jax.numpy as jnp
 from jax import lax
+from jax.experimental import pallas as pl
+from jax.experimental.pallas import tpu as pltpu
 from jax.sharding import PartitionSpec as P
 
 H = 8
@@ -132,6 +135,318 @@
     return (output, grad_tokens, grad_w_qkv, grad_w_out)
 
 
+MESH = pl.DeviceIdType.MESH
+CHUNKS = 4
+
+
+class Place:
+    def __init__(self, fsdp_size):
+        self.d, self.f = lax.axis_index("dp"), lax.axis_index("fsdp")
+        self.c = lax.rem(self.d, 2)
+        chip = lax.div(self.d, 2)
+        self.x, self.y = lax.rem(chip, 2), lax.div(chip, 2)
+        self.dx = self.dp_of(self.y, 1 - self.x, self.c)
+        self.dy = self.dp_of(1 - self.y, self.x, self.c)
+        self.dd = self.dp_of(1 - self.y, 1 - self.x, self.c)
+        self.dc = self.dp_of(self.y, self.x, 1 - self.c)
+        self.n = fsdp_size
+
+    def dp_of(self, y, x, c):
+        return (y * 2 + x) * 2 + c
+
+    def ahead(self, j):
+        return lax.rem(self.f + j, self.n)
+
+    def behind(self, j):
+        return lax.rem(self.f + self.n - j, self.n)
+
+    def barrier(self):
+        sem = pltpu.get_barrier_semaphore()
+        targets = [(self.dx, self.f), (self.dy, self.f), (self.dc, self.f)]
+        targets += [(self.d, self.ahead(j)) for j in range(1, self.n)]
+        for target in targets:
+            pl.semaphore_signal(sem, inc=1, device_id=target, device_id_type=MESH)
+        pl.semaphore_wait(sem, len(targets))
+
+
+def remote(src, dst, send_sem, recv_sem, target):
+    return pltpu.make_async_remote_copy(
+        src_ref=src,
+        dst_ref=dst,
+        send_sem=send_sem,
+        recv_sem=recv_sem,
+        device_id=target,
+        device_id_type=MESH,
+    )
+
+
+def gather_kernel(n, wq_ref, wo_ref, fq_ref, fo_ref, send, recv, local_sem):
+    me = Place(n)
+    rows = wq_ref.shape[0]
+    share = rows // 8
+    half = share // 2
+    mine, whole = (wq_ref, wo_ref), (fq_ref, fo_ref)
+    me.barrier()
+    started = {}
+
+    def span(a, f, d, first, count):
+        start = pl.multiple_of(f * rows + d * share + first, half)
+        return whole[a].at[pl.ds(start, count)]
+
+    def push(a, kind, j, f, d, first, count, target):
+        spot = span(a, f, d, first, count)
+        source = spot
+        if kind == 0:
+            source = mine[a].at[pl.ds(pl.multiple_of(d * share, share), share)]
+        slot = kind * (n - 1) + j - 1
+        copy = remote(source, spot, send.at[a, slot], recv.at[a, slot], target)
+        copy.start()
+        started[a, kind, j] = copy
+
+    for j in range(1, n):
+        for a in range(2):
+            push(a, 0, j, me.f, me.d, 0, share, (me.d, me.ahead(j)))
+    locals_ = []
+    for a in range(2):
+        start = pl.multiple_of(me.f * rows, rows)
+        copy = pltpu.make_async_copy(mine[a], whole[a].at[pl.ds(start, rows)], local_sem.at[a])
+        copy.start()
+        locals_.append(copy)
+
+    for step in range(1, n + 2):
+        for a in range(2):
+            j = step
+            if j < n:
+                f = me.behind(j)
+                started[a, 0, j].wait_recv()
+                push(a, 1, j, f, me.d, 0, share, (me.dx, me.f))
+                push(a, 2, j, f, me.d, 0, share, (me.dy, me.f))
+                push(a, 5, j, f, me.d, 0, share, (me.dc, me.f))
+            j = step - 1
+            if 1 <= j < n:
+                f = me.behind(j)
+                started[a, 1, j].wait_recv()
+                push(a, 3, j, f, me.dx, 0, half, (me.dy, me.f))
+                push(a, 6, j, f, me.dx, 0, share, (me.dc, me.f))
+                started[a, 2, j].wait_recv()
+                push(a, 4, j, f, me.dy, half, half, (me.dx, me.f))
+                push(a, 7, j, f, me.dy, 0, share, (me.dc, me.f))
+            j = step - 2
+            if 1 <= j < n:
+                f = me.behind(j)
+                started[a, 3, j].wait_recv()
+                push(a, 8, j, f, me.dd, 0, half, (me.dc, me.f))
+                started[a, 4, j].wait_recv()
+                push(a, 9, j, f, me.dd, half, half, (me.dc, me.f))
+    for (a, kind, j), copy in started.items():
+        copy.wait_send()
+        if kind >= 5:
+            copy.wait_recv()
+    for copy in locals_:
+        copy.wait()
+
+
+def gather_weights(n, w_qkv, w_out):
+    vmem = pl.BlockSpec(memory_space=pltpu.VMEM)
+    return pl.pallas_call(
+        functools.partial(gather_kernel, n),
+        out_shape=[
+            jax.ShapeDtypeStruct((w.shape[0] * n, w.shape[1]), w.dtype) for w in (w_qkv, w_out)
+        ],
+        in_specs=[vmem, vmem],
+        out_specs=[pl.BlockSpec(memory_space=pl.ANY)] * 2,
+        scratch_shapes=[
+            pltpu.SemaphoreType.DMA((2, 10 * (n - 1))),
+            pltpu.SemaphoreType.DMA((2, 10 * (n - 1))),
+            pltpu.SemaphoreType.DMA((2,)),
+        ],
+        compiler_params=pltpu.CompilerParams(collective_id=0, has_side_effects=True),
+        name="gather_weights",
+    )(w_qkv, w_out)
+
+
+def add_half(left, right):
+    return left.astype(jnp.float32) + right.astype(jnp.float32)
+
+
+def reduce_kernel(n, first_ref, second_ref, out_ref, core_sum, pair_sum, plane_sum, z_terms, send, recv):
+    me = Place(n)
+    width = second_ref.shape[-1]
+    share = second_ref.shape[-2]
+    half = share // 2
+    me.barrier()
+    started = {}
+
+    def source(k):
+        if k == CHUNKS - 1:
+            return second_ref, pl.ds(0, width)
+        return first_ref, pl.ds(k * width, width)
+
+    def push(k, kind, src, dst, target):
+        copy = remote(src, dst, send.at[k, kind], recv.at[k, kind], target)
+        copy.start()
+        started[k, kind] = copy
+
+    def columns(k):
+        return pl.ds(k * width, width)
+
+    def core_start(k):
+        ref, cols = source(k)
+        push(k, 0, ref.at[:, :, :, 1 - me.c, :, cols], core_sum.at[k], (me.dc, me.f))
+
+    def stage_core(k):
+        ref, cols = source(k)
+        started[k, 0].wait_recv()
+
+        def add(i, carry):
+            f, y, x = lax.div(i, 4), lax.rem(lax.div(i, 2), 2), lax.rem(i, 2)
+            total = add_half(ref[f, y, x, me.c, :, cols], core_sum[k, f, y, x])
+            core_sum[k, f, y, x] = total.astype(jnp.bfloat16)
+            return carry
+
+        lax.fori_loop(0, n * 4, add, 0)
+        if k % 2 == 0:
+            push(k, 1, core_sum.at[k, :, :, 1 - me.x], pair_sum.at[k], (me.dx, me.f))
+        else:
+            push(k, 1, core_sum.at[k, :, 1 - me.y], pair_sum.at[k], (me.dy, me.f))
+
+    def stage_pair(k):
+        started[k, 1].wait_recv()
+
+        def add(i, carry):
+            f, other = lax.div(i, 2), lax.rem(i, 2)
+            own = core_sum[k, f, other, me.x] if k % 2 == 0 else core_sum[k, f, me.y, other]
+            pair_sum[k, f, other] = add_half(own, pair_sum[k, f, other]).astype(jnp.bfloat16)
+            return carry
+
+        lax.fori_loop(0, n * 2, add, 0)
+        if k % 2 == 0:
+            push(k, 2, pair_sum.at[k, :, 1 - me.y], plane_sum.at[k], (me.dy, me.f))
+        else:
+            push(k, 2, pair_sum.at[k, :, 1 - me.x], plane_sum.at[k], (me.dx, me.f))
+
+    def stage_plane(k):
+        started[k, 2].wait_recv()
+        keep = me.y if k % 2 == 0 else me.x
+
+        def add(f, carry):
+            plane_sum[k, f] = add_half(pair_sum[k, f, keep], plane_sum[k, f]).astype(jnp.bfloat16)
+            return carry
+
+        lax.fori_loop(0, n, add, 0)
+        for j in range(1, n):
+            push(k, 2 + j, plane_sum.at[k, me.ahead(j)], z_terms.at[k, j - 1], (me.d, me.ahead(j)))
+
+    base = 2 + n
+
+    def stage_z(k):
+        total = plane_sum[k, me.f].astype(jnp.float32)
+        for j in range(1, n):
+            started[k, 2 + j].wait_recv()
+            total = total + z_terms[k, j - 1].astype(jnp.float32)
+        out_ref[me.d, :, columns(k)] = total.astype(jnp.bfloat16)
+        spot = out_ref.at[me.d, :, columns(k)]
+        push(k, base, spot, spot, (me.dx, me.f))
+        push(k, base + 1, spot, spot, (me.dy, me.f))
+        push(k, base + 4, spot, spot, (me.dc, me.f))
+
+    def stage_spread(k):
+        started[k, base].wait_recv()
+        spot = out_ref.at[me.dx, pl.ds(0, half), columns(k)]
+        push(k, base + 2, spot, spot, (me.dy, me.f))
+        spot = out_ref.at[me.dx, :, columns(k)]
+        push(k, base + 5, spot, spot, (me.dc, me.f))
+        started[k, base + 1].wait_recv()
+        spot = out_ref.at[me.dy, pl.ds(half, half), columns(k)]
+        push(k, base + 3, spot, spot, (me.dx, me.f))
+        spot = out_ref.at[me.dy, :, columns(k)]
+        push(k, base + 6, spot, spot, (me.dc, me.f))
+
+    def stage_last(k):
+        started[k, base + 2].wait_recv()
+        spot = out_ref.at[me.dd, pl.ds(0, half), columns(k)]
+        push(k, base + 7, spot, spot, (me.dc, me.f))
+        started[k, base + 3].wait_recv()
+        spot = out_ref.at[me.dd, pl.ds(half, half), columns(k)]
+        push(k, base + 8, spot, spot, (me.dc, me.f))
+
+    order = [CHUNKS - 1] + list(range(CHUNKS - 1))
+    for k in order:
+        core_start(k)
+    stages = [stage_core, stage_pair, stage_plane, stage_z, stage_spread, stage_last]
+    for step in range(CHUNKS + len(stages) - 1):
+        for s in reversed(range(len(stages))):
+            if 0 <= step - s < CHUNKS:
+                stages[s](order[step - s])
+    for (k, kind), copy in started.items():
+        copy.wait_send()
+        if kind >= base + 4:
+            copy.wait_recv()
+
+
+def reduce_grads(n, first_term, second_term):
+    share = first_term.shape[0] // (n * 8)
+    width = second_term.shape[1]
+    kinds = 2 + n + 9
+    views = [g.reshape(n, 2, 2, 2, share, g.shape[1]) for g in (first_term, second_term)]
+    vmem = pl.BlockSpec(memory_space=pltpu.VMEM)
+    return pl.pallas_call(
+        functools.partial(reduce_kernel, n),
+        out_shape=jax.ShapeDtypeStruct((8, share, CHUNKS * width), jnp.bfloat16),
+        in_specs=[vmem, vmem],
+        out_specs=vmem,
+        scratch_shapes=[
+            pltpu.VMEM((CHUNKS, n, 2, 2, share, width), jnp.bfloat16),
+            pltpu.VMEM((CHUNKS, n, 2, share, width), jnp.bfloat16),
+            pltpu.VMEM((CHUNKS, n, share, width), jnp.bfloat16),
+            pltpu.VMEM((CHUNKS, n - 1, share, width), jnp.bfloat16),
+            pltpu.SemaphoreType.DMA((CHUNKS, kinds)),
+            pltpu.SemaphoreType.DMA((CHUNKS, kinds)),
+        ],
+        compiler_params=pltpu.CompilerParams(
+            collective_id=1, has_side_effects=True, vmem_limit_bytes=48 << 20
+        ),
+        name="reduce_grads",
+    )(*views)
+
+
+def chip_body(tokens, w_qkv, w_out, doc_blocks, cotangent):
+    row_count = tokens.shape[0]
+    head_width = w_out.shape[1]
+    n = lax.axis_size("fsdp")
+    all_devices = lax.axis_size("dp") * n
+    allowed = row_mask(doc_blocks[0], row_count)
+    full_qkv, full_out = gather_weights(n, w_qkv, w_out)
+    qkv = jnp.dot(tokens, full_qkv, preferred_element_type=jnp.float32).astype(jnp.bfloat16)
+    query_rows = qkv[:, :head_width]
+    key_rows = qkv[:, head_width : 2 * head_width]
+    value_rows = qkv[:, 2 * head_width :]
+    mixed, attn_probs, probs_half = attend_forward(query_rows, key_rows, value_rows, allowed, H)
+    output = lax.dot_general(
+        mixed, full_out, CONTRACT_COLS, preferred_element_type=jnp.float32
+    ).astype(jnp.bfloat16)
+    grad_mixed = jnp.dot(cotangent, full_out, preferred_element_type=jnp.float32)
+    grad_mixed = grad_mixed.astype(jnp.bfloat16)
+    grad_qkv = attend_backward(
+        query_rows, key_rows, value_rows, attn_probs, probs_half, grad_mixed, H
+    )
+    grad_tokens = lax.dot_general(
+        grad_qkv, full_qkv, CONTRACT_COLS, preferred_element_type=jnp.float32
+    ).astype(jnp.bfloat16)
+    first_term = lax.dot_general(
+        tokens, grad_qkv, CONTRACT_ROWS, preferred_element_type=jnp.float32
+    ).astype(jnp.bfloat16)
+    second_term = lax.dot_general(
+        cotangent, mixed, CONTRACT_ROWS, preferred_element_type=jnp.float32
+    ).astype(jnp.bfloat16)
+    summed = reduce_grads(n, first_term, second_term)
+    summed = summed.reshape(w_out.shape[0], 4 * head_width).astype(jnp.float32)
+    norm_factor = 1.0 / math.sqrt(row_count * all_devices)
+    grad_w_qkv = summed[:, : 3 * head_width] * norm_factor
+    grad_w_out = summed[:, 3 * head_width :] * norm_factor
+    return (output, grad_tokens, grad_w_qkv, grad_w_out)
+
+
 def solution(mesh):
     placed = (
         P(("dp", "fsdp"), None),
@@ -140,8 +455,9 @@
         P(("dp", "fsdp"), None),
         P(("dp", "fsdp"), None),
     )
+    in_plane = mesh.shape["dp"] == 8 and mesh.shape["fsdp"] == 4
     return jax.shard_map(
-        body,
+        chip_body if in_plane else body,
         mesh=mesh,
         in_specs=placed,
         out_specs=(

time: 597 us -> 206 us (0.35)
  waiting for transfers between devices: 510 us -> 0 us
  Pallas kernels: 0 us -> 149 us
  between operations: 14 us -> 0.79 us
  local copies, waits for them, and re-layouts: 14.3 us -> 3.87 us
  other arithmetic: 17.8 us -> 9.06 us
    reduce_scatter x1 -> x0, waiting for transfers between devices: 279 us -> none  [body(): lax.psum_scatter(jnp.concatenate([first_term, second_term], axis=1), 'fsd...]
    all_gather x2 -> x0, waiting for transfers between devices: 156 us -> none  [the longest x1 111 us: body(): lax.all_gather(w_qkv, 'fsdp', axis=0, tiled=True)]
    pallas_call x0 -> x2, Pallas kernels: none -> 149 us  [the longest x1 99.9 us: reduce_grads(): pl.pallas_call(functools.partial(reduce_kernel, n), out_shape=jax.ShapeDt...]
    psum x1 -> x0, waiting for transfers between devices: 73.3 us -> none  [body(): summed = lax.psum(partial_grad, 'dp')]
    concatenate x1 -> x0, other arithmetic: 7.23 us -> none  [body(): jnp.concatenate([first_term, second_term], axis=1)]
  transfers between devices with their start and end apart: 4 -> 0, of which waited for: 4 -> 0; matrix products, arithmetic and copies ran while one was open for 3% -> 0% of each run, Pallas kernels for 0% -> 0%
where the time goes in v1:
time: 206 us
  Pallas kernels  149 us (72%)
  matrix products  43.3 us (21%)
  other arithmetic  9.06 us (4%)
  local copies, waits for them, and re-layouts  3.87 us (2%)
    pallas_call x1, Pallas kernels, reduce_grads(): pl.pallas_call(functools.partial(reduce_kernel, n), out_shape=jax.ShapeDt...  99.9 us
    pallas_call x1, Pallas kernels, gather_weights(): pl.pallas_call(functools.partial(gather_kernel, n), out_shape=[jax.ShapeD...  49.3 us
    dot_general x1, matrix products, chip_body(): lax.dot_general(tokens, grad_qkv, CONTRACT_ROWS, preferred_element_type=j...  8.65 us
    dot_general x1, matrix products, chip_body(): lax.dot_general(grad_qkv, full_qkv, CONTRACT_COLS, preferred_element_type...  7.29 us
    dot_general x1, matrix products, chip_body(): jnp.dot(tokens, full_qkv, preferred_element_type=jnp.float32)  6.62 us
    sub x1, matrix products, attend_forward(): expvals = jnp.exp(scores - highest)  5.43 us
    dot_general x1, matrix products, attend_forward(): jnp.einsum('hqk,khd->qhd', probs_half, value_heads, preferred_element_typ...  4.58 us

profile of v1, /device:TPU:0, one launch (start us, length us, event | category | flops | bytes accessed | tf_op | source)
XLA Modules:
  0.0 206.2 jit_solution(14196057720390061788)
XLA Ops:
  0.6 0.0 copy-start
  0.6 49.3 %gather_weights.1 = (bf16[1024,3072]{1,0:T(8,128)(2,1)}, bf16[1024,1024]{1,0:T(8,128)(2,1)}) custom-call(bf16[256,3072]{1,0:T(8,128)(2,1)} %wq_ref.1, bf16[256,1024]{1,0:T(8,128)(2,1)} %wo_ref.1), custom_call_target="tpu_custom_call" | custom-call | tf_op jit(solution)/shard_map/gather_weights/pallas_call | solution.py:251
  50.0 0.0 copy-done
  50.0 6.6 %fusion.5 = bf16[512,3072]{0,1:T(8,128)(2,1)S(1)} fusion(bf16[1024,3072]{1,0:T(8,128)(2,1)} %get-tuple-element.18, bf16[512,1024]{1,0:T(8,128)(2,1)S(1)} %copy-done), kind=kOutput, calls=%fused_computation.12 | convolution fusion | flops 3222798336 | bytes 10485760 | tf_op jit(solution)/shard_map/dot_general | solution.py:420
  56.6 0.0 copy-start.3
  56.6 1.2 fusion.25
  57.8 0.0 copy-done.3
  57.8 0.6 fusion.26
  58.4 2.6 %compare_select_fusion.1 = s32[512,1]{0,1:T(1,128)S(1)} fusion(s32[512,1]{0,1:T(1,128)S(1)} %bitcast.78, s32[512,1]{0,1:T(1,128)S(1)} %bitcast.79, s32[]{:T(128)} %bitcast.6, s32[]{:T(128)} %bitcast.7, s32[]{:T(128)} %bitcast.9, s32[]{:T(128)} %bitcast.8), kind=kLoop, calls=%fused_computation.33 | loop fusion | flops 4096 | bytes 6160 | tf_op jit(solution)/shard_map/jit(_take)/gather | solution.py:21
  61.0 0.2 fusion.16
  61.2 5.4 %fusion.27 = (f32[8,512]{1,0:T(8,128)S(1)}, f32[8,512,512]{1,2,0:T(8,128)}) fusion(pred[512,512]{0,1:T(8,128)(4,1)S(1)} %fusion.16, bf16[512,8,128]{0,2,1:T(8,128)(2,1)S(1)} %bitcast.70, bf16[512,8,128]{0,2,1:T(8,128)(2,1)S(1)} %bitcast.68), kind=kOutput, calls=%fused_computation.47 | convolution fusion | flops 545260032 | bytes 10764288 | tf_op jit(solution)/shard_map/sub | solution.py:43
  66.6 0.0 copy-start.4
  66.6 4.6 %fusion.10 = bf16[8,128,512]{2,1,0:T(8,128)(2,1)S(1)} fusion(bf16[512,8,128]{0,2,1:T(8,128)(2,1)} %bitcast.72, f32[8,512,512]{1,2,0:T(8,128)} %get-tuple-element.28, f32[8,512]{1,0:T(8,128)S(1)} %get-tuple-element.27), kind=kOutput, calls=%fused_computation.23 | convolution fusion | flops 541589504 | bytes 10502144 | tf_op jit(solution)/shard_map/hqk,khd->qhd/dot_general | solution.py:46
  71.2 0.0 copy-done.4
  71.2 0.0 copy-start.5
  71.2 2.3 %convolution_convert_fusion.4 = bf16[512,1024]{1,0:T(8,128)(2,1)} fusion(bf16[512,1024]{0,1:T(8,128)(2,1)S(1)} %bitcast.81, bf16[1024,1024]{1,0:T(8,128)(2,1)S(1)} %copy-done.4), kind=kOutput, calls=%fused_computation.26 | convolution fusion | flops 1074266112 | bytes 4194304 | tf_op jit(solution)/shard_map/dot_general | solution.py:425
  73.5 0.0 copy-done.5
  73.5 0.0 copy-start.1
  73.5 1.3 convolution_convert_fusion.3
  74.8 2.1 %copy-done.1 = f32[8,512,512]{1,2,0:T(8,128)S(1)} copy-done((f32[8,512,512]{1,2,0:T(8,128)S(1)}, f32[8,512,512]{1,2,0:T(8,128)}, u32[]{:S(2)}) %copy-start.1) | copy-done | bytes 8388632
  76.9 0.0 copy-start.2
  76.9 1.5 fusion.13
  78.4 0.0 copy-done.2
  78.4 2.1 %multiply_reduce_fusion = (f32[8,512]{1,0:T(8,128)S(1)}, f32[8,512,512]{1,2,0:T(8,128)S(1)}) fusion(f32[8,512,512]{1,2,0:T(8,128)S(1)} %copy-done.1, f32[8,512]{1,0:T(8,128)S(1)} %get-tuple-element.27, bf16[512,8,128]{0,2,1:T(8,128)(2,1)S(1)} %bitcast.86, bf16[512,8,128]{0,2,1:T(8,128)(2,1)S(1)} %bitcast.73), kind=kOutput, calls=%fused_computation.2 | convolution fusion | flops 543158272 | bytes 18907136 | tf_op jit(solution)/shard_map/qhd,khd->hqk/dot_general | solution.py:59
  80.5 2.7 %multiply_convert_fusion = bf16[8,512,512]{1,2,0:T(8,128)(2,1)S(1)} fusion(f32[8,512,512]{1,2,0:T(8,128)S(1)} %get-tuple-element.30, f32[8,512]{1,0:T(8,128)S(1)} %get-tuple-element.29, f32[8,512,512]{1,2,0:T(8,128)S(1)} %copy-done.1, f32[8,512]{1,0:T(8,128)S(1)} %get-tuple-element.27), kind=kLoop, calls=%fused_computation.1 | loop fusion | flops 8388608 | bytes 21004288 | tf_op jit(solution)/shard_map/convert_element_type | solution.py:66
  83.2 1.5 multiply_convert_fusion.1
  84.7 0.7 multiply_convert_fusion.2
  85.4 7.3 %convolution_convert_fusion.5 = bf16[512,1024]{1,0:T(8,128)(2,1)} fusion(bf16[1024,3072]{1,0:T(8,128)(2,1)} %get-tuple-element.18, bf16[512,1024]{0,1:T(8,128)(2,1)S(1)} %bitcast.83, bf16[512,1024]{0,1:T(8,128)(2,1)S(1)} %bitcast.74, bf16[512,1024]{0,1:T(8,128)(2,1)S(1)} %bitcast.76), kind=kOutput, calls=%fused_computation.27 | convolution fusion | flops 3231186944 | bytes 10485760 | tf_op jit(solution)/shard_map/dot_general | solution.py:433
  92.7 8.7 %convolution_convert_fusion = bf16[3072,1024]{0,1:T(8,128)(2,1)} fusion(bf16[512,1024]{1,0:T(8,128)(2,1)S(1)} %copy-done, bf16[512,1024]{0,1:T(8,128)(2,1)S(1)} %bitcast.84, bf16[512,1024]{0,1:T(8,128)(2,1)S(1)} %bitcast.75, bf16[512,1024]{0,1:T(8,128)(2,1)S(1)} %bitcast.77), kind=kOutput, calls=%fused_computation.6 | convolution fusion | flops 3233808384 | bytes 10485760 | tf_op jit(solution)/shard_map/dot_general | solution.py:436
  101.4 1.3 convolution_convert_fusion.2
  102.7 99.9 %reduce_grads.1 = bf16[8,32,4096]{2,1,0:T(8,128)(2,1)S(1)} custom-call(bf16[4,2,2,2,32,3072]{5,4,3,2,1,0:T(8,128)(2,1)} %bitcast.67, bf16[4,2,2,2,32,1024]{5,4,3,2,1,0:T(8,128)(2,1)S(1)} %bitcast.66), custom_call_target="tpu_custom_call" | custom-call | tf_op jit(solution)/shard_map/reduce_grads/pallas_call | solution.py:393
  202.6 0.6 bitcast_convert_fusion
  203.2 1.9 slice_multiply_fusion
  205.1 1.0 slice_multiply_fusion.1
  (3 shorter events, 0.0 us)
Async XLA Ops:
  0.6 49.3 %copy-start = (bf16[512,1024]{1,0:T(8,128)(2,1)S(1)}, bf16[512,1024]{1,0:T(8,128)(2,1)}, u32[]{:S(2)}) copy-start(bf16[512,1024]{1,0:T(8,128)(2,1)} %param.7) | copy-start | bytes 3145732
  56.6 1.2 copy-start.3
  66.6 4.6 %copy-start.4 = (bf16[1024,1024]{1,0:T(8,128)(2,1)S(1)}, bf16[1024,1024]{1,0:T(8,128)(2,1)}, u32[]{:S(2)}) copy-start(bf16[1024,1024]{1,0:T(8,128)(2,1)} %get-tuple-element.19) | copy-start | bytes 6291460
  71.2 2.3 %copy-start.5 = (bf16[512,1024]{1,0:T(8,128)(2,1)S(1)}, bf16[512,1024]{1,0:T(8,128)(2,1)}, u32[]{:S(2)}) copy-start(bf16[512,1024]{1,0:T(8,128)(2,1)} %param.11) | copy-start | bytes 3145732
  73.5 3.4 %copy-start.1 = (f32[8,512,512]{1,2,0:T(8,128)S(1)}, f32[8,512,512]{1,2,0:T(8,128)}, u32[]{:S(2)}) copy-start(f32[8,512,512]{1,2,0:T(8,128)} %get-tuple-element.28) | copy-start | bytes 25165828
  76.9 1.5 copy-start.2

commit v2 on v1

--- a/solution.py
+++ b/solution.py
@@ -180,7 +180,7 @@
     )
 
 
-def gather_kernel(n, wq_ref, wo_ref, fq_ref, fo_ref, send, recv, local_sem):
+def gather_kernel(n, wq_ref, wo_ref, t_ref, c_ref, fq_ref, fo_ref, tt_ref, ct_ref, send, recv, local_sem):
     me = Place(n)
     rows = wq_ref.shape[0]
     share = rows // 8
@@ -213,6 +213,13 @@
         copy.start()
         locals_.append(copy)
 
+    def turn(i, carry):
+        part = pl.ds(pl.multiple_of(i * 128, 128), 128)
+        tt_ref[part, :] = t_ref[:, part].T
+        ct_ref[part, :] = c_ref[:, part].T
+        return carry
+
+    lax.fori_loop(0, t_ref.shape[1] // 128, turn, 0)
     for step in range(1, n + 2):
         for a in range(2):
             j = step
@@ -246,15 +253,16 @@
         copy.wait()
 
 
-def gather_weights(n, w_qkv, w_out):
+def gather_weights(n, w_qkv, w_out, tokens, cotangent):
     vmem = pl.BlockSpec(memory_space=pltpu.VMEM)
     return pl.pallas_call(
         functools.partial(gather_kernel, n),
         out_shape=[
             jax.ShapeDtypeStruct((w.shape[0] * n, w.shape[1]), w.dtype) for w in (w_qkv, w_out)
-        ],
-        in_specs=[vmem, vmem],
-        out_specs=[pl.BlockSpec(memory_space=pl.ANY)] * 2,
+        ]
+        + [jax.ShapeDtypeStruct(t.shape[::-1], t.dtype) for t in (tokens, cotangent)],
+        in_specs=[vmem] * 4,
+        out_specs=[pl.BlockSpec(memory_space=pl.ANY)] * 2 + [vmem] * 2,
         scratch_shapes=[
             pltpu.SemaphoreType.DMA((2, 10 * (n - 1))),
             pltpu.SemaphoreType.DMA((2, 10 * (n - 1))),
@@ -262,25 +270,70 @@
         ],
         compiler_params=pltpu.CompilerParams(collective_id=0, has_side_effects=True),
         name="gather_weights",
-    )(w_qkv, w_out)
+    )(w_qkv, w_out, tokens, cotangent)
 
 
 def add_half(left, right):
     return left.astype(jnp.float32) + right.astype(jnp.float32)
 
 
-def reduce_kernel(n, first_ref, second_ref, out_ref, core_sum, pair_sum, plane_sum, z_terms, send, recv):
+def reduce_kernel(
+    n,
+    tt_ref,
+    ct_ref,
+    grad_ref,
+    mixed_ref,
+    fq_ref,
+    fo_ref,
+    sum_ref,
+    out_ref,
+    grad_tokens_ref,
+    wq,
+    wo,
+    grads,
+    core_sum,
+    pair_sum,
+    plane_sum,
+    z_terms,
+    send,
+    recv,
+    local_sem,
+):
     me = Place(n)
-    width = second_ref.shape[-1]
-    share = second_ref.shape[-2]
+    width = mixed_ref.shape[-1]
+    share = grads.shape[-2]
     half = share // 2
+    loads = []
+    for i, (src, dst) in enumerate(((fq_ref, wq), (fo_ref, wo))):
+        copy = pltpu.make_async_copy(src, dst, local_sem.at[i])
+        copy.start()
+        loads.append(copy)
     me.barrier()
     started = {}
 
-    def source(k):
-        if k == CHUNKS - 1:
-            return second_ref, pl.ds(0, width)
-        return first_ref, pl.ds(k * width, width)
+    def weight_grad(k):
+        def rows_of(f, carry):
+            rows = pl.ds(pl.multiple_of(f * share * 8, share * 8), share * 8)
+            if k == CHUNKS - 1:
+                left, right = ct_ref[rows, :], mixed_ref[...]
+            else:
+                left, right = tt_ref[rows, :], grad_ref[:, k * width : (k + 1) * width]
+            part = jnp.dot(left, right, preferred_element_type=jnp.float32)
+            grads[k, f] = part.astype(jnp.bfloat16).reshape(2, 2, 2, share, width)
+            return carry
+
+        lax.fori_loop(0, n, rows_of, 0)
+
+    def times_weights(left_ref, weight, target_ref):
+        def columns_of(i, carry):
+            cols = pl.ds(pl.multiple_of(i * 256, 256), 256)
+            part = lax.dot_general(
+                left_ref[...], weight[cols, :], CONTRACT_COLS, preferred_element_type=jnp.float32
+            )
+            target_ref[:, cols] = part.astype(jnp.bfloat16)
+            return carry
+
+        lax.fori_loop(0, weight.shape[0] // 256, columns_of, 0)
 
     def push(k, kind, src, dst, target):
         copy = remote(src, dst, send.at[k, kind], recv.at[k, kind], target)
@@ -291,16 +344,14 @@
         return pl.ds(k * width, width)
 
     def core_start(k):
-        ref, cols = source(k)
-        push(k, 0, ref.at[:, :, :, 1 - me.c, :, cols], core_sum.at[k], (me.dc, me.f))
+        push(k, 0, grads.at[k, :, :, :, 1 - me.c], core_sum.at[k], (me.dc, me.f))
 
     def stage_core(k):
-        ref, cols = source(k)
         started[k, 0].wait_recv()
 
         def add(i, carry):
             f, y, x = lax.div(i, 4), lax.rem(lax.div(i, 2), 2), lax.rem(i, 2)
-            total = add_half(ref[f, y, x, me.c, :, cols], core_sum[k, f, y, x])
+            total = add_half(grads[k, f, y, x, me.c], core_sum[k, f, y, x])
             core_sum[k, f, y, x] = total.astype(jnp.bfloat16)
             return carry
 
@@ -344,70 +395,102 @@
         for j in range(1, n):
             started[k, 2 + j].wait_recv()
             total = total + z_terms[k, j - 1].astype(jnp.float32)
-        out_ref[me.d, :, columns(k)] = total.astype(jnp.bfloat16)
-        spot = out_ref.at[me.d, :, columns(k)]
+        sum_ref[me.d, :, columns(k)] = total.astype(jnp.bfloat16)
+        spot = sum_ref.at[me.d, :, columns(k)]
         push(k, base, spot, spot, (me.dx, me.f))
         push(k, base + 1, spot, spot, (me.dy, me.f))
         push(k, base + 4, spot, spot, (me.dc, me.f))
 
     def stage_spread(k):
         started[k, base].wait_recv()
-        spot = out_ref.at[me.dx, pl.ds(0, half), columns(k)]
+        spot = sum_ref.at[me.dx, pl.ds(0, half), columns(k)]
         push(k, base + 2, spot, spot, (me.dy, me.f))
-        spot = out_ref.at[me.dx, :, columns(k)]
+        spot = sum_ref.at[me.dx, :, columns(k)]
         push(k, base + 5, spot, spot, (me.dc, me.f))
         started[k, base + 1].wait_recv()
-        spot = out_ref.at[me.dy, pl.ds(half, half), columns(k)]
+        spot = sum_ref.at[me.dy, pl.ds(half, half), columns(k)]
         push(k, base + 3, spot, spot, (me.dx, me.f))
-        spot = out_ref.at[me.dy, :, columns(k)]
+        spot = sum_ref.at[me.dy, :, columns(k)]
         push(k, base + 6, spot, spot, (me.dc, me.f))
 
     def stage_last(k):
         started[k, base + 2].wait_recv()
-        spot = out_ref.at[me.dd, pl.ds(0, half), columns(k)]
+        spot = sum_ref.at[me.dd, pl.ds(0, half), columns(k)]
         push(k, base + 7, spot, spot, (me.dc, me.f))
         started[k, base + 3].wait_recv()
-        spot = out_ref.at[me.dd, pl.ds(half, half), columns(k)]
+        spot = sum_ref.at[me.dd, pl.ds(half, half), columns(k)]
         push(k, base + 8, spot, spot, (me.dc, me.f))
 
     order = [CHUNKS - 1] + list(range(CHUNKS - 1))
-    for k in order:
-        core_start(k)
-    stages = [stage_core, stage_pair, stage_plane, stage_z, stage_spread, stage_last]
-    for step in range(CHUNKS + len(stages) - 1):
-        for s in reversed(range(len(stages))):
-            if 0 <= step - s < CHUNKS:
-                stages[s](order[step - s])
+    weight_grad(order[0])
+    for before, k in zip(order, order[1:]):
+        weight_grad(k)
+        core_start(before)
+        if before != order[0]:
+            stage_core(order[order.index(before) - 1])
+    core_start(order[-1])
+    stage_core(order[-2])
+    stage_core(order[-1])
+    for copy in loads:
+        copy.wait()
+    times_weights(grad_ref, wq, grad_tokens_ref)
+    first, second = order[: CHUNKS // 2], order[CHUNKS // 2 :]
+    for k in first:
+        stage_pair(k)
+    times_weights(mixed_ref, wo, out_ref)
+    plan = [
+        (stage_plane, first),
+        (stage_pair, second),
+        (stage_z, first),
+        (stage_plane, second),
+        (stage_spread, first),
+        (stage_z, second),
+        (stage_last, first),
+        (stage_spread, second),
+        (stage_last, second),
+    ]
+    for stage, group in plan:
+        for k in group:
+            stage(k)
     for (k, kind), copy in started.items():
         copy.wait_send()
         if kind >= base + 4:
             copy.wait_recv()
 
 
-def reduce_grads(n, first_term, second_term):
-    share = first_term.shape[0] // (n * 8)
-    width = second_term.shape[1]
+def reduce_grads(n, tokens_t, cotangent_t, grad_qkv, mixed, full_qkv, full_out):
+    features, rows = tokens_t.shape
+    share = features // (n * 8)
+    width = mixed.shape[1]
     kinds = 2 + n + 9
-    views = [g.reshape(n, 2, 2, 2, share, g.shape[1]) for g in (first_term, second_term)]
     vmem = pl.BlockSpec(memory_space=pltpu.VMEM)
+    anywhere = pl.BlockSpec(memory_space=pl.ANY)
     return pl.pallas_call(
         functools.partial(reduce_kernel, n),
-        out_shape=jax.ShapeDtypeStruct((8, share, CHUNKS * width), jnp.bfloat16),
-        in_specs=[vmem, vmem],
-        out_specs=vmem,
+        out_shape=[
+            jax.ShapeDtypeStruct((8, share, CHUNKS * width), jnp.bfloat16),
+            jax.ShapeDtypeStruct((rows, features), jnp.bfloat16),
+            jax.ShapeDtypeStruct((rows, features), jnp.bfloat16),
+        ],
+        in_specs=[vmem] * 4 + [anywhere] * 2,
+        out_specs=[vmem] * 3,
         scratch_shapes=[
+            pltpu.VMEM(full_qkv.shape, jnp.bfloat16),
+            pltpu.VMEM(full_out.shape, jnp.bfloat16),
+            pltpu.VMEM((CHUNKS, n, 2, 2, 2, share, width), jnp.bfloat16),
             pltpu.VMEM((CHUNKS, n, 2, 2, share, width), jnp.bfloat16),
             pltpu.VMEM((CHUNKS, n, 2, share, width), jnp.bfloat16),
             pltpu.VMEM((CHUNKS, n, share, width), jnp.bfloat16),
             pltpu.VMEM((CHUNKS, n - 1, share, width), jnp.bfloat16),
             pltpu.SemaphoreType.DMA((CHUNKS, kinds)),
             pltpu.SemaphoreType.DMA((CHUNKS, kinds)),
+            pltpu.SemaphoreType.DMA((2,)),
         ],
         compiler_params=pltpu.CompilerParams(
-            collective_id=1, has_side_effects=True, vmem_limit_bytes=48 << 20
+            collective_id=1, has_side_effects=True, vmem_limit_bytes=54 << 20
         ),
         name="reduce_grads",
-    )(*views)
+    )(tokens_t, cotangent_t, grad_qkv, mixed, full_qkv, full_out)
 
 
 def chip_body(tokens, w_qkv, w_out, doc_blocks, cotangent):
@@ -416,30 +499,22 @@
     n = lax.axis_size("fsdp")
     all_devices = lax.axis_size("dp") * n
     allowed = row_mask(doc_blocks[0], row_count)
-    full_qkv, full_out = gather_weights(n, w_qkv, w_out)
+    full_qkv, full_out, tokens_t, cotangent_t = gather_weights(
+        n, w_qkv, w_out, tokens, cotangent
+    )
     qkv = jnp.dot(tokens, full_qkv, preferred_element_type=jnp.float32).astype(jnp.bfloat16)
     query_rows = qkv[:, :head_width]
     key_rows = qkv[:, head_width : 2 * head_width]
     value_rows = qkv[:, 2 * head_width :]
     mixed, attn_probs, probs_half = attend_forward(query_rows, key_rows, value_rows, allowed, H)
-    output = lax.dot_general(
-        mixed, full_out, CONTRACT_COLS, preferred_element_type=jnp.float32
-    ).astype(jnp.bfloat16)
     grad_mixed = jnp.dot(cotangent, full_out, preferred_element_type=jnp.float32)
     grad_mixed = grad_mixed.astype(jnp.bfloat16)
     grad_qkv = attend_backward(
         query_rows, key_rows, value_rows, attn_probs, probs_half, grad_mixed, H
     )
-    grad_tokens = lax.dot_general(
-        grad_qkv, full_qkv, CONTRACT_COLS, preferred_element_type=jnp.float32
-    ).astype(jnp.bfloat16)
-    first_term = lax.dot_general(
-        tokens, grad_qkv, CONTRACT_ROWS, preferred_element_type=jnp.float32
-    ).astype(jnp.bfloat16)
-    second_term = lax.dot_general(
-        cotangent, mixed, CONTRACT_ROWS, preferred_element_type=jnp.float32
-    ).astype(jnp.bfloat16)
-    summed = reduce_grads(n, first_term, second_term)
+    summed, output, grad_tokens = reduce_grads(
+        n, tokens_t, cotangent_t, grad_qkv, mixed, full_qkv, full_out
+    )
     summed = summed.reshape(w_out.shape[0], 4 * head_width).astype(jnp.float32)
     norm_factor = 1.0 / math.sqrt(row_count * all_devices)
     grad_w_qkv = summed[:, : 3 * head_width] * norm_factor

time: 206 us -> 191 us (0.927)
  Pallas kernels: 149 us -> 133 us
  matrix products: 43.3 us -> 31.7 us
  other arithmetic: 9.06 us -> 15.2 us
  local copies, waits for them, and re-layouts: 3.87 us -> 9.22 us
    dot_general x4 -> x0, matrix products: 19.5 us -> none  [the longest x1 8.65 us: chip_body(): lax.dot_general(tokens, grad_qkv, CONTRACT_ROWS, preferred_element_type=j...]
    pallas_call x1, Pallas kernels: 99.9 us -> 81.8 us  [reduce_grads(): pl.pallas_call(functools.partial(reduce_kernel, n), out_shape=[jax.ShapeD...]
    reshape x0 -> x4, local copies, waits for them, and re-layouts: none -> 4.67 us  [the longest x3 3.33 us: attend_backward(): p.astype(jnp.bfloat16).reshape(row_count, -1)]
    dot_general x1, matrix products: 1.49 us -> 5.21 us  [attend_backward(): jnp.einsum('hqk,qhd->khd', probs_half, grad_heads, preferred_element_type...]
    dot_general x1, matrix products: 2.07 us -> 5.34 us  [attend_backward(): jnp.einsum('qhd,khd->hqk', grad_heads, value_heads, preferred_element_typ...]
    concatenate x0 -> x1, other arithmetic: none -> 2.82 us  [attend_backward(): jnp.concatenate([p.astype(jnp.bfloat16).reshape(row_count, -1) for p in p...]
    dot_general x1, matrix products: 1.3 us -> 4.01 us  [chip_body(): jnp.dot(cotangent, full_out, preferred_element_type=jnp.float32)]
    dot_general x1, matrix products: 6.62 us -> 4.03 us  [chip_body(): jnp.dot(tokens, full_qkv, preferred_element_type=jnp.float32)]
where the time goes in v2:
time: 191 us; the launch traced here: 190 us
  Pallas kernels  133 us (70%)
  matrix products  31.7 us (17%)
  other arithmetic  15.2 us (8%)
  local copies, waits for them, and re-layouts  9.22 us (5%)
    pallas_call x1, Pallas kernels, reduce_grads(): pl.pallas_call(functools.partial(reduce_kernel, n), out_shape=[jax.ShapeD...  81.8 us
    pallas_call x1, Pallas kernels, gather_weights(): pl.pallas_call(functools.partial(gather_kernel, n), out_shape=[jax.ShapeD...  51.2 us
    sub x1, matrix products, attend_forward(): expvals = jnp.exp(scores - highest)  5.39 us
    dot_general x1, matrix products, attend_backward(): jnp.einsum('qhd,khd->hqk', grad_heads, value_heads, preferred_element_typ...  5.34 us
    dot_general x1, matrix products, attend_backward(): jnp.einsum('hqk,qhd->khd', probs_half, grad_heads, preferred_element_type...  5.21 us
    convert_element_type x1, other arithmetic, attend_backward(): grad_scores = (attn_probs * (grad_probs - inner)).astype(jnp.bfloat16)  4.5 us
    dot_general x1, matrix products, attend_forward(): jnp.einsum('hqk,khd->qhd', probs_half, value_heads, preferred_element_typ...  4.45 us
    dot_general x1, matrix products, chip_body(): jnp.dot(tokens, full_qkv, preferred_element_type=jnp.float32)  4.03 us

profile of v2, /device:TPU:0, one launch (start us, length us, event | category | flops | bytes accessed | tf_op | source)
XLA Modules:
  0.0 189.8 jit_solution(1288268382862997756)
XLA Ops:
  0.6 0.0 copy-start.5
  0.7 1.4 fusion.24
  2.1 2.6 %compare_select_fusion.1 = s32[512,1]{0,1:T(1,128)S(1)} fusion(s32[512,1]{0,1:T(1,128)S(1)} %bitcast.65, s32[512,1]{0,1:T(1,128)S(1)} %bitcast.64, s32[]{:T(128)} %bitcast.6, s32[]{:T(128)} %bitcast.7, s32[]{:T(128)} %bitcast.9, s32[]{:T(128)} %bitcast.8), kind=kLoop, calls=%fused_computation.29 | loop fusion | flops 4096 | bytes 6160 | tf_op jit(solution)/shard_map/jit(_take)/gather | solution.py:21
  4.7 0.2 fusion.16
  4.9 51.2 %gather_weights.1 = (bf16[1024,3072]{1,0:T(8,128)(2,1)}, bf16[1024,1024]{1,0:T(8,128)(2,1)}, bf16[1024,512]{1,0:T(8,128)(2,1)}, bf16[1024,512]{1,0:T(8,128)(2,1)}) custom-call(bf16[256,3072]{1,0:T(8,128)(2,1)} %wq_ref.1, bf16[256,1024]{1,0:T(8,128)(2,1)} %wo_ref.1, bf16[512,1024]{1,0:T(8,128)(2,1)} %t_ref.1, bf16[512,1024]{1,0:T(8,128)(2,1)} %c_ref.1), custom_call_target="tpu_custom_call" | custom-call | tf_op jit(solution)/shard_map/gather_weights/pallas_call | solution.py:258
  56.1 0.0 copy-done.5
  56.1 0.0 copy-start
  56.1 0.0 copy-start.6
  56.1 4.0 %convolution_convert_fusion.1 = bf16[1024,512]{1,0:T(8,128)(2,1)} fusion(bf16[1024,1024]{1,0:T(8,128)(2,1)} %get-tuple-element.26.fo_ref, bf16[512,1024]{1,0:T(8,128)(2,1)S(1)} %copy-done.5), kind=kOutput, calls=%fused_computation.23 | convolution fusion | flops 1074266112 | bytes 4194304 | tf_op jit(solution)/shard_map/dot_general | solution.py:510
  60.2 0.0 copy-done
  60.2 0.0 copy-done.6
  60.2 4.0 %fusion.5 = bf16[512,3072]{0,1:T(8,128)(2,1)S(1)} fusion(bf16[1024,3072]{1,0:T(8,128)(2,1)S(1)} %copy-done, bf16[512,1024]{1,0:T(8,128)(2,1)S(1)} %copy-done.6), kind=kOutput, calls=%fused_computation.11 | convolution fusion | flops 3222798336 | bytes 10485760 | tf_op jit(solution)/shard_map/dot_general | solution.py:505
  64.2 1.2 fusion.23
  65.4 0.0 copy-start.1
  65.4 5.4 %fusion.25 = (f32[8,512]{1,0:T(8,128)S(1)}, f32[8,512,512]{1,2,0:T(8,128)}) fusion(pred[512,512]{0,1:T(8,128)(4,1)S(1)} %fusion.16, bf16[512,8,128]{0,2,1:T(8,128)(2,1)S(1)} %bitcast.58, bf16[512,8,128]{0,2,1:T(8,128)(2,1)S(1)} %bitcast.56), kind=kOutput, calls=%fused_computation.41 | convolution fusion | flops 545260032 | bytes 10764288 | tf_op jit(solution)/shard_map/sub | solution.py:43
  70.8 0.0 copy-done.1
  70.8 5.2 %fusion.10 = bf16[8,128,512]{2,1,0:T(8,128)(2,1)S(1)} fusion(bf16[512,8,128]{0,2,1:T(8,128)(2,1)} %bitcast.67, f32[8,512,512]{1,2,0:T(8,128)} %get-tuple-element.38, f32[8,512]{1,0:T(8,128)S(1)} %get-tuple-element.37), kind=kOutput, calls=%fused_computation.21 | convolution fusion | flops 541589504 | bytes 10502144 | tf_op jit(solution)/shard_map/hqk,qhd->khd/dot_general | solution.py:62
  76.0 0.5 copy.31
  76.5 4.4 %fusion.13 = bf16[8,128,512]{2,1,0:T(8,128)(2,1)S(1)} fusion(bf16[512,8,128]{0,2,1:T(8,128)(2,1)} %bitcast.62, f32[8,512,512]{1,2,0:T(8,128)} %get-tuple-element.38, f32[8,512]{1,0:T(8,128)S(1)} %get-tuple-element.37), kind=kOutput, calls=%fused_computation.22 | convolution fusion | flops 541589504 | bytes 10502144 | tf_op jit(solution)/shard_map/hqk,khd->qhd/dot_general | solution.py:46
  81.0 1.3 copy.32.mixed_ref
  82.3 5.3 %multiply_reduce_fusion = (f32[8,512]{1,0:T(8,128)S(1)}, f32[8,512,512]{1,2,0:T(8,128)S(1)}) fusion(f32[8,512,512]{1,2,0:T(8,128)} %get-tuple-element.38, f32[8,512]{1,0:T(8,128)S(1)} %get-tuple-element.37, bf16[512,8,128]{0,2,1:T(8,128)(2,1)} %bitcast.68, bf16[512,8,128]{0,2,1:T(8,128)(2,1)} %bitcast.63), kind=kOutput, calls=%fused_computation.2 | convolution fusion | flops 543158272 | bytes 18907136 | tf_op jit(solution)/shard_map/qhd,khd->hqk/dot_general | solution.py:59
  87.7 0.0 copy-start.2
  87.7 4.5 %multiply_convert_fusion = bf16[8,512,512]{1,2,0:T(8,128)(2,1)S(1)} fusion(f32[8,512,512]{1,2,0:T(8,128)S(1)} %get-tuple-element.40, f32[8,512]{1,0:T(8,128)S(1)} %get-tuple-element.39, f32[8,512,512]{1,2,0:T(8,128)} %get-tuple-element.38, f32[8,512]{1,0:T(8,128)S(1)} %get-tuple-element.37), kind=kLoop, calls=%fused_computation.1 | loop fusion | flops 8388608 | bytes 21004288 | tf_op jit(solution)/shard_map/convert_element_type | solution.py:66
  92.2 0.0 copy-done.2
  92.2 1.5 multiply_convert_fusion.1
  93.7 1.7 multiply_convert_fusion.2
  95.4 1.5 copy.29
  96.9 1.3 copy.30
  98.3 2.8 %pad_maximum_fusion.grad_ref = bf16[512,3072]{1,0:T(8,128)(2,1)} fusion(bf16[512,1024]{1,0:T(8,128)(2,1)S(1)} %copy.31, bf16[512,1024]{1,0:T(8,128)(2,1)} %copy.30, bf16[512,1024]{1,0:T(8,128)(2,1)S(1)} %copy.29), kind=kLoop, calls=%fused_computation.13 | loop fusion | flops 9437184 | bytes 6291456 | tf_op jit(solution)/shard_map/concatenate | solution.py:76
  101.1 81.8 %reduce_grads.1 = (bf16[8,32,4096]{2,1,0:T(8,128)(2,1)}, bf16[512,1024]{1,0:T(8,128)(2,1)}, bf16[512,1024]{1,0:T(8,128)(2,1)}) custom-call(bf16[1024,512]{1,0:T(8,128)(2,1)} %get-tuple-element.23.tt_ref, bf16[1024,512]{1,0:T(8,128)(2,1)} %get-tuple-element.24.ct_ref, bf16[512,3072]{1,0:T(8,128)(2,1)} %pad_maximum_fusion.grad_ref, ...), custom_call_target="tpu_custom_call" | custom-call | tf_op jit(solution)/shard_map/reduce_grads/pallas_call | solution.py:468
  182.9 2.1 %bitcast_convert_fusion = f32[256,4096]{1,0:T(8,128)S(1)} fusion(bf16[8,32,4096]{2,1,0:T(8,128)(2,1)} %get-tuple-element.29), kind=kLoop, calls=%fused_computation.14 | loop fusion | flops 1048576 | bytes 6291456 | tf_op jit(solution)/shard_map/convert_element_type | solution.py:518
  184.9 0.0 copy-start.4
  184.9 1.1 slice_multiply_fusion.1
  186.0 0.0 copy-start.3
  186.0 1.9 %slice_multiply_fusion = f32[256,3072]{1,0:T(8,128)} fusion(f32[256,4096]{1,0:T(8,128)S(1)} %bitcast_convert_fusion), kind=kLoop, calls=%fused_computation.12 | loop fusion | flops 786432 | bytes 6291456 | tf_op jit(solution)/shard_map/mul | solution.py:520
  187.9 0.0 copy-done.4
  187.9 1.0 copy.35
  188.9 0.0 copy-done.3
  188.9 1.0 copy.36
  (3 shorter events, 0.0 us)
Async XLA Ops:
  0.6 55.5 %copy-start.5 = (bf16[512,1024]{1,0:T(8,128)(2,1)S(1)}, bf16[512,1024]{1,0:T(8,128)(2,1)}, u32[]{:S(2)}) copy-start(bf16[512,1024]{1,0:T(8,128)(2,1)} %c_ref.1) | copy-start | bytes 3145732
  56.1 4.0 %copy-start = (bf16[1024,3072]{1,0:T(8,128)(2,1)S(1)}, bf16[1024,3072]{1,0:T(8,128)(2,1)}, u32[]{:S(2)}) copy-start(bf16[1024,3072]{1,0:T(8,128)(2,1)} %get-tuple-element.25.fq_ref) | copy-start | bytes 18874372
  56.1 4.0 %copy-start.6 = (bf16[512,1024]{1,0:T(8,128)(2,1)S(1)}, bf16[512,1024]{1,0:T(8,128)(2,1)}, u32[]{:S(2)}) copy-start(bf16[512,1024]{1,0:T(8,128)(2,1)} %t_ref.1) | copy-start | bytes 3145732
  65.4 5.4 %copy-start.1 = (bf16[512,1024]{0,1:T(8,128)(2,1)}, bf16[512,1024]{0,1:T(8,128)(2,1)S(1)}, u32[]{:S(2)}) copy-start(bf16[512,1024]{0,1:T(8,128)(2,1)S(1)} %get-tuple-element.31) | copy-start | bytes 3145732
  87.7 4.5 %copy-start.2 = (bf16[512,1024]{0,1:T(8,128)(2,1)S(1)}, bf16[512,1024]{0,1:T(8,128)(2,1)}, u32[]{:S(2)}) copy-start(bf16[512,1024]{0,1:T(8,128)(2,1)} %copy-done.1) | copy-start | bytes 3145732
  184.9 3.0 %copy-start.4 = (bf16[512,1024]{1,0:T(8,128)(2,1)S(1)}, bf16[512,1024]{1,0:T(8,128)(2,1)}, u32[]{:S(2)}) copy-start(bf16[512,1024]{1,0:T(8,128)(2,1)} %get-tuple-element.45) | copy-start | bytes 3145732
  186.0 2.9 %copy-start.3 = (bf16[512,1024]{1,0:T(8,128)(2,1)S(1)}, bf16[512,1024]{1,0:T(8,128)(2,1)}, u32[]{:S(2)}) copy-start(bf16[512,1024]{1,0:T(8,128)(2,1)} %get-tuple-element.46) | copy-start | bytes 3145732

commit v3 on v2

--- a/solution.py
+++ b/solution.py
@@ -136,7 +136,7 @@
 
 
 MESH = pl.DeviceIdType.MESH
-CHUNKS = 4
+CHUNKS = 8
 
 
 class Place:
@@ -300,7 +300,7 @@
     local_sem,
 ):
     me = Place(n)
-    width = mixed_ref.shape[-1]
+    width = 4 * mixed_ref.shape[-1] // CHUNKS
     share = grads.shape[-2]
     half = share // 2
     loads = []
@@ -314,26 +314,24 @@
     def weight_grad(k):
         def rows_of(f, carry):
             rows = pl.ds(pl.multiple_of(f * share * 8, share * 8), share * 8)
-            if k == CHUNKS - 1:
-                left, right = ct_ref[rows, :], mixed_ref[...]
+            first = k * width
+            if first >= grad_ref.shape[1]:
+                first -= grad_ref.shape[1]
+                left, right = ct_ref[rows, :], mixed_ref[:, first : first + width]
             else:
-                left, right = tt_ref[rows, :], grad_ref[:, k * width : (k + 1) * width]
+                left, right = tt_ref[rows, :], grad_ref[:, first : first + width]
             part = jnp.dot(left, right, preferred_element_type=jnp.float32)
             grads[k, f] = part.astype(jnp.bfloat16).reshape(2, 2, 2, share, width)
             return carry
 
         lax.fori_loop(0, n, rows_of, 0)
 
-    def times_weights(left_ref, weight, target_ref):
-        def columns_of(i, carry):
-            cols = pl.ds(pl.multiple_of(i * 256, 256), 256)
-            part = lax.dot_general(
-                left_ref[...], weight[cols, :], CONTRACT_COLS, preferred_element_type=jnp.float32
-            )
-            target_ref[:, cols] = part.astype(jnp.bfloat16)
-            return carry
-
-        lax.fori_loop(0, weight.shape[0] // 256, columns_of, 0)
+    def times_weights(left_ref, weight, target_ref, i):
+        cols = pl.ds(i * 256, 256)
+        part = lax.dot_general(
+            left_ref[...], weight[cols, :], CONTRACT_COLS, preferred_element_type=jnp.float32
+        )
+        target_ref[:, cols] = part.astype(jnp.bfloat16)
 
     def push(k, kind, src, dst, target):
         copy = remote(src, dst, send.at[k, kind], recv.at[k, kind], target)
@@ -421,37 +419,30 @@
         spot = sum_ref.at[me.dd, pl.ds(half, half), columns(k)]
         push(k, base + 8, spot, spot, (me.dc, me.f))
 
-    order = [CHUNKS - 1] + list(range(CHUNKS - 1))
-    weight_grad(order[0])
-    for before, k in zip(order, order[1:]):
-        weight_grad(k)
-        core_start(before)
-        if before != order[0]:
-            stage_core(order[order.index(before) - 1])
-    core_start(order[-1])
-    stage_core(order[-2])
-    stage_core(order[-1])
-    for copy in loads:
-        copy.wait()
-    times_weights(grad_ref, wq, grad_tokens_ref)
-    first, second = order[: CHUNKS // 2], order[CHUNKS // 2 :]
-    for k in first:
-        stage_pair(k)
-    times_weights(mixed_ref, wo, out_ref)
-    plan = [
-        (stage_plane, first),
-        (stage_pair, second),
-        (stage_z, first),
-        (stage_plane, second),
-        (stage_spread, first),
-        (stage_z, second),
-        (stage_last, first),
-        (stage_spread, second),
-        (stage_last, second),
-    ]
-    for stage, group in plan:
-        for k in group:
-            stage(k)
+    order = [CHUNKS - 1, CHUNKS - 2] + list(range(CHUNKS - 2))
+    stages = (
+        (0, weight_grad),
+        (1, core_start),
+        (2, stage_core),
+        (4, stage_pair),
+        (6, stage_plane),
+        (8, stage_z),
+        (9, stage_spread),
+        (10, stage_last),
+    )
+    pieces = [(grad_ref, wq, grad_tokens_ref, i) for i in range(wq.shape[0] // 256)]
+    pieces += [(mixed_ref, wo, out_ref, i) for i in range(wo.shape[0] // 256)]
+    for step in range(CHUNKS + 10):
+        for after, stage in stages:
+            if 0 <= step - after < CHUNKS:
+                stage(order[step - after])
+        if step == 2:
+            for copy in loads:
+                copy.wait()
+        if step >= 2 and pieces:
+            times_weights(*pieces.pop(0))
+    for piece in pieces:
+        times_weights(*piece)
     for (k, kind), copy in started.items():
         copy.wait_send()
         if kind >= base + 4:
@@ -461,7 +452,7 @@
 def reduce_grads(n, tokens_t, cotangent_t, grad_qkv, mixed, full_qkv, full_out):
     features, rows = tokens_t.shape
     share = features // (n * 8)
-    width = mixed.shape[1]
+    width = 4 * mixed.shape[1] // CHUNKS
     kinds = 2 + n + 9
     vmem = pl.BlockSpec(memory_space=pltpu.VMEM)
     anywhere = pl.BlockSpec(memory_space=pl.ANY)

time: 191 us -> 183 us (0.958)
  Pallas kernels: 133 us -> 126 us
    pallas_call x1, Pallas kernels: 81.8 us -> 75.1 us  [reduce_grads(): pl.pallas_call(functools.partial(reduce_kernel, n), out_shape=[jax.ShapeD...]
where the time goes in v3:
time: 183 us
  Pallas kernels  126 us (69%)
  matrix products  31.7 us (17%)
  other arithmetic  15.2 us (8%)
  local copies, waits for them, and re-layouts  9.22 us (5%)
    pallas_call x1, Pallas kernels, reduce_grads(): pl.pallas_call(functools.partial(reduce_kernel, n), out_shape=[jax.ShapeD...  75.1 us
    pallas_call x1, Pallas kernels, gather_weights(): pl.pallas_call(functools.partial(gather_kernel, n), out_shape=[jax.ShapeD...  51.2 us
    sub x1, matrix products, attend_forward(): expvals = jnp.exp(scores - highest)  5.39 us
    dot_general x1, matrix products, attend_backward(): jnp.einsum('qhd,khd->hqk', grad_heads, value_heads, preferred_element_typ...  5.34 us
    dot_general x1, matrix products, attend_backward(): jnp.einsum('hqk,qhd->khd', probs_half, grad_heads, preferred_element_type...  5.21 us
    convert_element_type x1, other arithmetic, attend_backward(): grad_scores = (attn_probs * (grad_probs - inner)).astype(jnp.bfloat16)  4.5 us
    dot_general x1, matrix products, attend_forward(): jnp.einsum('hqk,khd->qhd', probs_half, value_heads, preferred_element_typ...  4.45 us
    dot_general x1, matrix products, chip_body(): jnp.dot(tokens, full_qkv, preferred_element_type=jnp.float32)  4.03 us

profile of v3, /device:TPU:0, one launch (start us, length us, event | category | flops | bytes accessed | tf_op | source)
XLA Modules:
  0.0 183.2 jit_solution(13354452353467773232)
XLA Ops:
  0.6 0.0 copy-start.5
  0.7 1.4 fusion.24
  2.1 2.6 %compare_select_fusion.1 = s32[512,1]{0,1:T(1,128)S(1)} fusion(s32[512,1]{0,1:T(1,128)S(1)} %bitcast.65, s32[512,1]{0,1:T(1,128)S(1)} %bitcast.64, s32[]{:T(128)} %bitcast.6, s32[]{:T(128)} %bitcast.7, s32[]{:T(128)} %bitcast.9, s32[]{:T(128)} %bitcast.8), kind=kLoop, calls=%fused_computation.29 | loop fusion | flops 4096 | bytes 6160 | tf_op jit(solution)/shard_map/jit(_take)/gather | solution.py:21
  4.7 0.2 fusion.16
  4.9 51.2 %gather_weights.1 = (bf16[1024,3072]{1,0:T(8,128)(2,1)}, bf16[1024,1024]{1,0:T(8,128)(2,1)}, bf16[1024,512]{1,0:T(8,128)(2,1)}, bf16[1024,512]{1,0:T(8,128)(2,1)}) custom-call(bf16[256,3072]{1,0:T(8,128)(2,1)} %wq_ref.1, bf16[256,1024]{1,0:T(8,128)(2,1)} %wo_ref.1, bf16[512,1024]{1,0:T(8,128)(2,1)} %t_ref.1, bf16[512,1024]{1,0:T(8,128)(2,1)} %c_ref.1), custom_call_target="tpu_custom_call" | custom-call | tf_op jit(solution)/shard_map/gather_weights/pallas_call | solution.py:258
  56.1 0.0 copy-done.5
  56.1 0.0 copy-start
  56.1 0.0 copy-start.6
  56.1 4.0 %convolution_convert_fusion.1 = bf16[1024,512]{1,0:T(8,128)(2,1)} fusion(bf16[1024,1024]{1,0:T(8,128)(2,1)} %get-tuple-element.26.fo_ref, bf16[512,1024]{1,0:T(8,128)(2,1)S(1)} %copy-done.5), kind=kOutput, calls=%fused_computation.23 | convolution fusion | flops 1074266112 | bytes 4194304 | tf_op jit(solution)/shard_map/dot_general | solution.py:501
  60.2 0.0 copy-done
  60.2 0.0 copy-done.6
  60.2 4.0 %fusion.5 = bf16[512,3072]{0,1:T(8,128)(2,1)S(1)} fusion(bf16[1024,3072]{1,0:T(8,128)(2,1)S(1)} %copy-done, bf16[512,1024]{1,0:T(8,128)(2,1)S(1)} %copy-done.6), kind=kOutput, calls=%fused_computation.11 | convolution fusion | flops 3222798336 | bytes 10485760 | tf_op jit(solution)/shard_map/dot_general | solution.py:496
  64.2 1.2 fusion.23
  65.4 0.0 copy-start.1
  65.4 5.4 %fusion.25 = (f32[8,512]{1,0:T(8,128)S(1)}, f32[8,512,512]{1,2,0:T(8,128)}) fusion(pred[512,512]{0,1:T(8,128)(4,1)S(1)} %fusion.16, bf16[512,8,128]{0,2,1:T(8,128)(2,1)S(1)} %bitcast.58, bf16[512,8,128]{0,2,1:T(8,128)(2,1)S(1)} %bitcast.56), kind=kOutput, calls=%fused_computation.41 | convolution fusion | flops 545260032 | bytes 10764288 | tf_op jit(solution)/shard_map/sub | solution.py:43
  70.8 0.0 copy-done.1
  70.8 5.2 %fusion.10 = bf16[8,128,512]{2,1,0:T(8,128)(2,1)S(1)} fusion(bf16[512,8,128]{0,2,1:T(8,128)(2,1)} %bitcast.67, f32[8,512,512]{1,2,0:T(8,128)} %get-tuple-element.38, f32[8,512]{1,0:T(8,128)S(1)} %get-tuple-element.37), kind=kOutput, calls=%fused_computation.21 | convolution fusion | flops 541589504 | bytes 10502144 | tf_op jit(solution)/shard_map/hqk,qhd->khd/dot_general | solution.py:62
  76.0 0.5 copy.31
  76.5 4.4 %fusion.13 = bf16[8,128,512]{2,1,0:T(8,128)(2,1)S(1)} fusion(bf16[512,8,128]{0,2,1:T(8,128)(2,1)} %bitcast.62, f32[8,512,512]{1,2,0:T(8,128)} %get-tuple-element.38, f32[8,512]{1,0:T(8,128)S(1)} %get-tuple-element.37), kind=kOutput, calls=%fused_computation.22 | convolution fusion | flops 541589504 | bytes 10502144 | tf_op jit(solution)/shard_map/hqk,khd->qhd/dot_general | solution.py:46
  81.0 1.3 copy.32.mixed_ref
  82.3 5.3 %multiply_reduce_fusion = (f32[8,512]{1,0:T(8,128)S(1)}, f32[8,512,512]{1,2,0:T(8,128)S(1)}) fusion(f32[8,512,512]{1,2,0:T(8,128)} %get-tuple-element.38, f32[8,512]{1,0:T(8,128)S(1)} %get-tuple-element.37, bf16[512,8,128]{0,2,1:T(8,128)(2,1)} %bitcast.68, bf16[512,8,128]{0,2,1:T(8,128)(2,1)} %bitcast.63), kind=kOutput, calls=%fused_computation.2 | convolution fusion | flops 543158272 | bytes 18907136 | tf_op jit(solution)/shard_map/qhd,khd->hqk/dot_general | solution.py:59
  87.7 0.0 copy-start.2
  87.7 4.5 %multiply_convert_fusion = bf16[8,512,512]{1,2,0:T(8,128)(2,1)S(1)} fusion(f32[8,512,512]{1,2,0:T(8,128)S(1)} %get-tuple-element.40, f32[8,512]{1,0:T(8,128)S(1)} %get-tuple-element.39, f32[8,512,512]{1,2,0:T(8,128)} %get-tuple-element.38, f32[8,512]{1,0:T(8,128)S(1)} %get-tuple-element.37), kind=kLoop, calls=%fused_computation.1 | loop fusion | flops 8388608 | bytes 21004288 | tf_op jit(solution)/shard_map/convert_element_type | solution.py:66
  92.2 0.0 copy-done.2
  92.2 1.5 multiply_convert_fusion.1
  93.7 1.7 multiply_convert_fusion.2
  95.4 1.5 copy.29
  96.9 1.3 copy.30
  98.3 2.8 %pad_maximum_fusion.grad_ref = bf16[512,3072]{1,0:T(8,128)(2,1)} fusion(bf16[512,1024]{1,0:T(8,128)(2,1)S(1)} %copy.31, bf16[512,1024]{1,0:T(8,128)(2,1)} %copy.30, bf16[512,1024]{1,0:T(8,128)(2,1)S(1)} %copy.29), kind=kLoop, calls=%fused_computation.13 | loop fusion | flops 9437184 | bytes 6291456 | tf_op jit(solution)/shard_map/concatenate | solution.py:76
  101.1 75.1 %reduce_grads.1 = (bf16[8,32,4096]{2,1,0:T(8,128)(2,1)}, bf16[512,1024]{1,0:T(8,128)(2,1)}, bf16[512,1024]{1,0:T(8,128)(2,1)}) custom-call(bf16[1024,512]{1,0:T(8,128)(2,1)} %get-tuple-element.23.tt_ref, bf16[1024,512]{1,0:T(8,128)(2,1)} %get-tuple-element.24.ct_ref, bf16[512,3072]{1,0:T(8,128)(2,1)} %pad_maximum_fusion.grad_ref, ...), custom_call_target="tpu_custom_call" | custom-call | tf_op jit(solution)/shard_map/reduce_grads/pallas_call | solution.py:459
  176.2 2.1 %bitcast_convert_fusion = f32[256,4096]{1,0:T(8,128)S(1)} fusion(bf16[8,32,4096]{2,1,0:T(8,128)(2,1)} %get-tuple-element.29), kind=kLoop, calls=%fused_computation.14 | loop fusion | flops 1048576 | bytes 6291456 | tf_op jit(solution)/shard_map/convert_element_type | solution.py:509
  178.3 0.0 copy-start.4
  178.3 1.1 slice_multiply_fusion.1
  179.3 0.0 copy-start.3
  179.3 1.9 %slice_multiply_fusion = f32[256,3072]{1,0:T(8,128)} fusion(f32[256,4096]{1,0:T(8,128)S(1)} %bitcast_convert_fusion), kind=kLoop, calls=%fused_computation.12 | loop fusion | flops 786432 | bytes 6291456 | tf_op jit(solution)/shard_map/mul | solution.py:511
  181.2 0.0 copy-done.4
  181.2 1.0 copy.35
  182.2 0.0 copy-done.3
  182.2 1.0 copy.36
  (3 shorter events, 0.0 us)
Async XLA Ops:
  0.6 55.5 %copy-start.5 = (bf16[512,1024]{1,0:T(8,128)(2,1)S(1)}, bf16[512,1024]{1,0:T(8,128)(2,1)}, u32[]{:S(2)}) copy-start(bf16[512,1024]{1,0:T(8,128)(2,1)} %c_ref.1) | copy-start | bytes 3145732
  56.1 4.0 %copy-start = (bf16[1024,3072]{1,0:T(8,128)(2,1)S(1)}, bf16[1024,3072]{1,0:T(8,128)(2,1)}, u32[]{:S(2)}) copy-start(bf16[1024,3072]{1,0:T(8,128)(2,1)} %get-tuple-element.25.fq_ref) | copy-start | bytes 18874372
  56.1 4.0 %copy-start.6 = (bf16[512,1024]{1,0:T(8,128)(2,1)S(1)}, bf16[512,1024]{1,0:T(8,128)(2,1)}, u32[]{:S(2)}) copy-start(bf16[512,1024]{1,0:T(8,128)(2,1)} %t_ref.1) | copy-start | bytes 3145732
  65.4 5.4 %copy-start.1 = (bf16[512,1024]{0,1:T(8,128)(2,1)}, bf16[512,1024]{0,1:T(8,128)(2,1)S(1)}, u32[]{:S(2)}) copy-start(bf16[512,1024]{0,1:T(8,128)(2,1)S(1)} %get-tuple-element.31) | copy-start | bytes 3145732
  87.7 4.5 %copy-start.2 = (bf16[512,1024]{0,1:T(8,128)(2,1)S(1)}, bf16[512,1024]{0,1:T(8,128)(2,1)}, u32[]{:S(2)}) copy-start(bf16[512,1024]{0,1:T(8,128)(2,1)} %copy-done.1) | copy-start | bytes 3145732
  178.3 3.0 %copy-start.4 = (bf16[512,1024]{1,0:T(8,128)(2,1)S(1)}, bf16[512,1024]{1,0:T(8,128)(2,1)}, u32[]{:S(2)}) copy-start(bf16[512,1024]{1,0:T(8,128)(2,1)} %get-tuple-element.45) | copy-start | bytes 3145732
  179.3 2.9 %copy-start.3 = (bf16[512,1024]{1,0:T(8,128)(2,1)S(1)}, bf16[512,1024]{1,0:T(8,128)(2,1)}, u32[]{:S(2)}) copy-start(bf16[512,1024]{1,0:T(8,128)(2,1)} %get-tuple-element.46) | copy-start | bytes 3145732

commit v4 on v3

--- a/solution.py
+++ b/solution.py
@@ -315,23 +315,28 @@
         def rows_of(f, carry):
             rows = pl.ds(pl.multiple_of(f * share * 8, share * 8), share * 8)
             first = k * width
-            if first >= grad_ref.shape[1]:
-                first -= grad_ref.shape[1]
+            part, first = divmod(first, mixed_ref.shape[1])
+            if part == 3:
                 left, right = ct_ref[rows, :], mixed_ref[:, first : first + width]
             else:
-                left, right = tt_ref[rows, :], grad_ref[:, first : first + width]
+                left, right = tt_ref[rows, :], grad_ref[part, :, first : first + width]
             part = jnp.dot(left, right, preferred_element_type=jnp.float32)
             grads[k, f] = part.astype(jnp.bfloat16).reshape(2, 2, 2, share, width)
             return carry
 
         lax.fori_loop(0, n, rows_of, 0)
 
-    def times_weights(left_ref, weight, target_ref, i):
+    def times_weights(lefts, weight, target_ref, i):
         cols = pl.ds(i * 256, 256)
-        part = lax.dot_general(
-            left_ref[...], weight[cols, :], CONTRACT_COLS, preferred_element_type=jnp.float32
-        )
-        target_ref[:, cols] = part.astype(jnp.bfloat16)
+        total = None
+        for p, left_ref in enumerate(lefts):
+            deep = left_ref.shape[1]
+            right = weight[cols, p * deep : (p + 1) * deep]
+            part = lax.dot_general(
+                left_ref[...], right, CONTRACT_COLS, preferred_element_type=jnp.float32
+            )
+            total = part if total is None else total + part
+        target_ref[:, cols] = total.astype(jnp.bfloat16)
 
     def push(k, kind, src, dst, target):
         copy = remote(src, dst, send.at[k, kind], recv.at[k, kind], target)
@@ -430,8 +435,9 @@
         (9, stage_spread),
         (10, stage_last),
     )
-    pieces = [(grad_ref, wq, grad_tokens_ref, i) for i in range(wq.shape[0] // 256)]
-    pieces += [(mixed_ref, wo, out_ref, i) for i in range(wo.shape[0] // 256)]
+    lefts = [grad_ref.at[p] for p in range(3)]
+    pieces = [(lefts, wq, grad_tokens_ref, i) for i in range(wq.shape[0] // 256)]
+    pieces += [([mixed_ref], wo, out_ref, i) for i in range(wo.shape[0] // 256)]
     for step in range(CHUNKS + 10):
         for after, stage in stages:
             if 0 <= step - after < CHUNKS:
@@ -484,6 +490,54 @@
     )(tokens_t, cotangent_t, grad_qkv, mixed, full_qkv, full_out)
 
 
+def attend_kernel(mask_ref, q_ref, k_ref, v_ref, gm_ref, mixed_ref, grad_ref):
+    q, k, v, gm = q_ref[...], k_ref[...], v_ref[...], gm_ref[...]
+    scale = q.shape[1] ** (-0.5)
+
+    def dot(left, right, dims):
+        return lax.dot_general(left, right, dims, preferred_element_type=jnp.float32)
+
+    plain = (((1,), (0,)), ((), ()))
+    scores = jnp.where(mask_ref[...] > 0.0, dot(q, k, CONTRACT_COLS) * scale, NEG_FILL)
+    expvals = jnp.exp(scores - jnp.max(scores, axis=-1, keepdims=True))
+    probs = expvals / jnp.sum(expvals, axis=-1, keepdims=True)
+    probs_half = probs.astype(jnp.bfloat16)
+    mixed_ref[...] = dot(probs_half, v, plain).astype(jnp.bfloat16)
+    grad_probs = dot(gm, v, CONTRACT_COLS)
+    inner = jnp.sum(probs * grad_probs, axis=-1, keepdims=True)
+    grad_scores = (probs * (grad_probs - inner)).astype(jnp.bfloat16)
+    grad_ref[0] = (dot(grad_scores, k, plain) * scale).astype(jnp.bfloat16)
+    grad_ref[1] = (dot(grad_scores, q, CONTRACT_ROWS) * scale).astype(jnp.bfloat16)
+    grad_ref[2] = dot(probs_half, gm, CONTRACT_ROWS).astype(jnp.bfloat16)
+
+
+def attend(mask, qkv, grad_mixed, head_count):
+    rows, width = grad_mixed.shape
+    size = width // head_count
+
+    def column(first):
+        return pl.BlockSpec((rows, size), lambda h: (0, first + h))
+
+    return pl.pallas_call(
+        attend_kernel,
+        grid=(head_count,),
+        out_shape=[
+            jax.ShapeDtypeStruct((rows, width), jnp.bfloat16),
+            jax.ShapeDtypeStruct((3, rows, width), jnp.bfloat16),
+        ],
+        in_specs=[
+            pl.BlockSpec((rows, rows), lambda h: (0, 0)),
+            column(0),
+            column(head_count),
+            column(2 * head_count),
+            column(0),
+        ],
+        out_specs=[column(0), pl.BlockSpec((3, rows, size), lambda h: (0, 0, h))],
+        compiler_params=pltpu.CompilerParams(vmem_limit_bytes=48 << 20),
+        name="attend",
+    )(mask, qkv, qkv, qkv, grad_mixed)
+
+
 def chip_body(tokens, w_qkv, w_out, doc_blocks, cotangent):
     row_count = tokens.shape[0]
     head_width = w_out.shape[1]
@@ -494,15 +548,9 @@
         n, w_qkv, w_out, tokens, cotangent
     )
     qkv = jnp.dot(tokens, full_qkv, preferred_element_type=jnp.float32).astype(jnp.bfloat16)
-    query_rows = qkv[:, :head_width]
-    key_rows = qkv[:, head_width : 2 * head_width]
-    value_rows = qkv[:, 2 * head_width :]
-    mixed, attn_probs, probs_half = attend_forward(query_rows, key_rows, value_rows, allowed, H)
     grad_mixed = jnp.dot(cotangent, full_out, preferred_element_type=jnp.float32)
     grad_mixed = grad_mixed.astype(jnp.bfloat16)
-    grad_qkv = attend_backward(
-        query_rows, key_rows, value_rows, attn_probs, probs_half, grad_mixed, H
-    )
+    mixed, grad_qkv = attend(allowed.astype(jnp.float32), qkv, grad_mixed, H)
     summed, output, grad_tokens = reduce_grads(
         n, tokens_t, cotangent_t, grad_qkv, mixed, full_qkv, full_out
     )

time: 183 us -> 163 us (0.89)
  matrix products: 31.7 us -> 7.76 us
  Pallas kernels: 126 us -> 142 us
  other arithmetic: 15.2 us -> 7.81 us
  local copies, waits for them, and re-layouts: 9.22 us -> 4.72 us
    dot_general x5 -> x0, matrix products: 18.2 us -> none  [the longest x1 5.34 us: attend_backward(): jnp.einsum('qhd,khd->hqk', grad_heads, value_heads, preferred_element_typ...]
    pallas_call x0 -> x1, Pallas kernels: none -> 15.3 us  [attend(): pl.pallas_call(attend_kernel, grid=(head_count,), out_shape=[jax.ShapeDty...]
    sub x1 -> x0, matrix products: 5.39 us -> none  [attend_forward(): expvals = jnp.exp(scores - highest)]
    reshape x4 -> x0, local copies, waits for them, and re-layouts: 4.67 us -> none  [the longest x3 3.33 us: attend_backward(): p.astype(jnp.bfloat16).reshape(row_count, -1)]
    convert_element_type x1, other arithmetic: 4.5 us -> 0.18 us  [chip_body(): mixed, grad_qkv = attend(allowed.astype(jnp.float32), qkv, grad_mixed, H)]
    concatenate x1 -> x0, other arithmetic: 2.82 us -> none  [attend_backward(): jnp.concatenate([p.astype(jnp.bfloat16).reshape(row_count, -1) for p in p...]
where the time goes in v4:
time: 163 us
  Pallas kernels  142 us (87%)
  other arithmetic  7.81 us (5%)
  matrix products  7.76 us (5%)
  local copies, waits for them, and re-layouts  4.72 us (3%)
    pallas_call x1, Pallas kernels, reduce_grads(): pl.pallas_call(functools.partial(reduce_kernel, n), out_shape=[jax.ShapeD...  75.2 us
    pallas_call x1, Pallas kernels, gather_weights(): pl.pallas_call(functools.partial(gather_kernel, n), out_shape=[jax.ShapeD...  51.3 us
    pallas_call x1, Pallas kernels, attend(): pl.pallas_call(attend_kernel, grid=(head_count,), out_shape=[jax.ShapeDty...  15.3 us
    dot_general x1, matrix products, chip_body(): jnp.dot(tokens, full_qkv, preferred_element_type=jnp.float32)  4.77 us
    unnamed x14, local copies, waits for them, and re-layouts  3.33 us

profile of v4, /device:TPU:0, one launch (start us, length us, event | category | flops | bytes accessed | tf_op | source)
XLA Modules:
  0.0 162.8 jit_solution(6402798261494071252)
XLA Ops:
  0.6 0.0 copy-start.4
  0.7 1.4 fusion.6
  2.1 2.6 %compare_select_fusion.1 = s32[512,1]{0,1:T(1,128)S(1)} fusion(s32[512,1]{0,1:T(1,128)S(1)} %bitcast.27, s32[512,1]{0,1:T(1,128)S(1)} %bitcast.26, s32[]{:T(128)} %bitcast.4, s32[]{:T(128)} %bitcast.5, s32[]{:T(128)} %bitcast.7, s32[]{:T(128)} %bitcast.6), kind=kLoop, calls=%fused_computation.11 | loop fusion | flops 4096 | bytes 6160 | tf_op jit(solution)/shard_map/jit(_take)/gather | solution.py:21
  4.7 0.2 fusion.3.mask_ref
  4.9 0.0 copy-start.5
  4.9 51.3 %gather_weights.1 = (bf16[1024,3072]{1,0:T(8,128)(2,1)}, bf16[1024,1024]{1,0:T(8,128)(2,1)}, bf16[1024,512]{1,0:T(8,128)(2,1)}, bf16[1024,512]{1,0:T(8,128)(2,1)}) custom-call(bf16[256,3072]{1,0:T(8,128)(2,1)} %wq_ref.1, bf16[256,1024]{1,0:T(8,128)(2,1)} %wo_ref.1, bf16[512,1024]{1,0:T(8,128)(2,1)} %t_ref.1, bf16[512,1024]{1,0:T(8,128)(2,1)} %c_ref.1), custom_call_target="tpu_custom_call" | custom-call | tf_op jit(solution)/shard_map/gather_weights/pallas_call | solution.py:258
  56.1 0.0 copy-done.4
  56.1 0.0 copy-start.1
  56.2 3.0 %fusion.1.gm_ref = bf16[512,1024]{1,0:T(8,128)(2,1)S(1)} fusion(bf16[512,1024]{1,0:T(8,128)(2,1)S(1)} %copy-done.4, bf16[1024,1024]{1,0:T(8,128)(2,1)} %get-tuple-element.28.fo_ref), kind=kOutput, calls=%fused_computation.5 | convolution fusion | flops 1074266112 | bytes 4194304 | tf_op jit(solution)/shard_map/dot_general | solution.py:551
  59.2 0.0 copy-done.5
  59.2 0.4 copy-done.1
  59.6 4.8 %fusion.q_ref.k_ref.v_ref = bf16[512,3072]{1,0:T(8,128)(2,1)} fusion(bf16[512,1024]{1,0:T(8,128)(2,1)S(1)} %copy-done.5, bf16[1024,3072]{1,0:T(8,128)(2,1)S(1)} %copy-done.1), kind=kOutput, calls=%fused_computation.1 | convolution fusion | flops 3222798336 | bytes 10485760 | tf_op jit(solution)/shard_map/dot_general | solution.py:550
  64.3 15.3 %attend.1 = (bf16[512,1024]{1,0:T(8,128)(2,1)S(1)}, bf16[3,512,1024]{2,1,0:T(8,128)(2,1)}) custom-call(f32[512,512]{1,0:T(8,128)S(1)} %fusion.3.mask_ref, bf16[512,3072]{1,0:T(8,128)(2,1)} %fusion.q_ref.k_ref.v_ref, bf16[512,3072]{1,0:T(8,128)(2,1)} %fusion.q_ref.k_ref.v_ref, bf16[512,3072]{1,0:T(8,128)(2,1)} %fusion.q_ref.k_ref.v_ref, ...), custom_call_target="tpu_custom_call" | custom-call | tf_op jit(solution)/shard_map/attend/pallas_call | solution.py:521
  79.6 0.0 copy-start
  79.6 1.0 copy-done
  80.6 75.2 %reduce_grads.1 = (bf16[8,32,4096]{2,1,0:T(8,128)(2,1)}, bf16[512,1024]{1,0:T(8,128)(2,1)}, bf16[512,1024]{1,0:T(8,128)(2,1)}) custom-call(bf16[1024,512]{1,0:T(8,128)(2,1)} %get-tuple-element.25.tt_ref, bf16[1024,512]{1,0:T(8,128)(2,1)} %get-tuple-element.26.ct_ref, bf16[3,512,1024]{2,1,0:T(8,128)(2,1)} %get-tuple-element.29.grad_ref, ...), custom_call_target="tpu_custom_call" | custom-call | tf_op jit(solution)/shard_map/reduce_grads/pallas_call | solution.py:465
  155.8 2.1 %bitcast_convert_fusion = f32[256,4096]{1,0:T(8,128)S(1)} fusion(bf16[8,32,4096]{2,1,0:T(8,128)(2,1)} %get-tuple-element.33), kind=kLoop, calls=%fused_computation.3 | loop fusion | flops 1048576 | bytes 6291456 | tf_op jit(solution)/shard_map/convert_element_type | solution.py:557
  157.9 1.1 slice_multiply_fusion.1
  158.9 0.0 copy-start.3
  158.9 0.0 copy-start.2
  158.9 1.9 %slice_multiply_fusion = f32[256,3072]{1,0:T(8,128)} fusion(f32[256,4096]{1,0:T(8,128)S(1)} %bitcast_convert_fusion), kind=kLoop, calls=%fused_computation.2 | loop fusion | flops 786432 | bytes 6291456 | tf_op jit(solution)/shard_map/mul | solution.py:559
  160.8 0.0 copy-done.3
  160.8 1.0 copy.15
  161.8 0.0 copy-done.2
  161.8 1.0 copy.16
  (3 shorter events, 0.0 us)
Async XLA Ops:
  0.6 55.5 %copy-start.4 = (bf16[512,1024]{1,0:T(8,128)(2,1)S(1)}, bf16[512,1024]{1,0:T(8,128)(2,1)}, u32[]{:S(2)}) copy-start(bf16[512,1024]{1,0:T(8,128)(2,1)} %c_ref.1) | copy-start | bytes 3145732
  4.9 54.3 %copy-start.5 = (bf16[512,1024]{1,0:T(8,128)(2,1)S(1)}, bf16[512,1024]{1,0:T(8,128)(2,1)}, u32[]{:S(2)}) copy-start(bf16[512,1024]{1,0:T(8,128)(2,1)} %t_ref.1) | copy-start | bytes 3145732
  56.1 3.4 %copy-start.1 = (bf16[1024,3072]{1,0:T(8,128)(2,1)S(1)}, bf16[1024,3072]{1,0:T(8,128)(2,1)}, u32[]{:S(2)}) copy-start(bf16[1024,3072]{1,0:T(8,128)(2,1)} %get-tuple-element.27.fq_ref) | copy-start | bytes 18874372
  79.6 1.0 copy-start
  158.9 1.9 %copy-start.3 = (bf16[512,1024]{1,0:T(8,128)(2,1)S(1)}, bf16[512,1024]{1,0:T(8,128)(2,1)}, u32[]{:S(2)}) copy-start(bf16[512,1024]{1,0:T(8,128)(2,1)} %get-tuple-element.42) | copy-start | bytes 3145732
  158.9 2.9 %copy-start.2 = (bf16[512,1024]{1,0:T(8,128)(2,1)S(1)}, bf16[512,1024]{1,0:T(8,128)(2,1)}, u32[]{:S(2)}) copy-start(bf16[512,1024]{1,0:T(8,128)(2,1)} %get-tuple-element.43) | copy-start | bytes 3145732
